TPU v7x, 512 devices: a whole 4x8x8 slice. The times are simulated.
512 devices in a mesh: gx: 32 (over x_lo, z, core), gy: 16 (over y, x_hi).
Axes of the slice: x: 4 (x_hi: 2, x_lo: 2; x = x_hi * 2 + x_lo), y: 8, z: 8, core: 2. Of those that a mesh axis runs over, the one named last changes fastest.
Arguments:
- currents: bfloat16 [1024, 512, 2, 128], P('gx', 'gy'), may hold values from -6 to 6
- box_count: int32 [1024, 512], P('gx', 'gy'), may hold values from 0 to 128, as said below
- aggregate: bfloat16 [256, 256], replicated, may hold values from -0.375 to 0.375
- near_blocks: bfloat16 [9, 256, 256], replicated, may hold values from -0.125 to 0.125
- low_translator: float32 [16, 2, 128], replicated, may hold values from -1.5 to 1.5
- child_to_parent: bfloat16 [4, 256, 512], replicated, may hold values from -0.1875 to 0.1875
- coarse_list: int32 [512, 256, 16], P('gx', 'gy'), may hold values from 0 to 4095
- coarse_kind: int32 [512, 256, 16], P('gx', 'gy'), may hold values from 0 to 63
- coarse_count: int32 [512, 256], P('gx', 'gy'), may hold values from 1 to 16, as said below
- up_translator: float32 [64, 2, 256], replicated, may hold values from -1.5 to 1.5
- parent_to_child: bfloat16 [4, 512, 256], replicated, may hold values from -0.25 to 0.25
- receive_map: bfloat16 [256, 256], replicated, may hold values from -0.375 to 0.375
Outputs:
- field: float32 [1024, 512, 2, 128], P('gx', 'gy')
Inputs may be any that keep to these rules, and one draw needn't show every extreme that they name: `box_count`: ground clutter makes some boxes full and most sparse; some box holds 128 unknowns and some none. `coarse_count`: some list uses all 16 entries.
All inputs are finite; a program needn't handle non-finite values.
Results may differ from a plain program's by a relative error of at most 0.0041.
Values may be sent and summed in bfloat16 or wider, within the bound.
A program may use at most 128 MiB of HBM per device.

v0:
```python
import jax
import jax.numpy as jnp
from jax import lax
from jax.sharding import PartitionSpec as P


def extended(cells, sides, width):
    for axis, dim in sides:
        count = lax.axis_size(axis)
        ends = count - 1
        head = lax.slice_in_dim(cells, 0, width, axis=dim)
        tail = lax.slice_in_dim(cells, cells.shape[dim] - width, cells.shape[dim], axis=dim)
        cells = jnp.concatenate(
            [
                lax.ppermute(tail, axis, [(i, (i + 1) % count) for i in range(ends)]),
                cells,
                lax.ppermute(head, axis, [((i + 1) % count, i) for i in range(ends)]),
            ],
            axis=dim,
        )
    return cells


def complex_flat(table, pattern, half):
    real_part = pattern[..., :half].astype(jnp.float32)
    imag_part = pattern[..., half:].astype(jnp.float32)
    first = table[..., :half] * real_part - table[..., half:] * imag_part
    second = table[..., :half] * imag_part + table[..., half:] * real_part
    return jnp.concatenate([first, second], axis=-1)


def make_patterns(block, aggregate):
    size_a, size_b = (block.shape[0], block.shape[1])
    flat_block = block.reshape(size_a * size_b, block.shape[2] * block.shape[3])
    result = jnp.dot(flat_block, aggregate, preferred_element_type=jnp.float32)
    return result.astype(jnp.bfloat16).reshape(size_a, size_b, aggregate.shape[1])


def translate_group(flat_group, lists, kinds, counts, table):
    rows_a, rows_b, slots = lists.shape
    kind_total, width_two = table.shape
    half = width_two // 2
    kind_ids = jnp.arange(kind_total, dtype=jnp.int32)[None, :]

    def accumulate(slot, total):
        index = lists[:, :, slot].reshape(rows_a * rows_b)
        source = jnp.take(flat_group, index, axis=0)
        choose = (kinds[:, :, slot].reshape(rows_a * rows_b)[:, None] == kind_ids).astype(
            jnp.float32
        )
        factors = jnp.dot(
            choose, table, precision=lax.Precision.HIGHEST, preferred_element_type=jnp.float32
        )
        term = complex_flat(factors, source, half)
        keep = (slot < counts).reshape(rows_a * rows_b)
        return total + jnp.where(keep[:, None], term, jnp.zeros_like(term))

    start = jnp.zeros((rows_a * rows_b, width_two), jnp.float32)
    result = lax.fori_loop(0, slots, accumulate, start)
    return result.astype(jnp.bfloat16).reshape(rows_a, rows_b, width_two)


def body(
    currents,
    box_count,
    aggregate,
    near_blocks,
    low_translator,
    child_to_parent,
    coarse_list,
    coarse_kind,
    coarse_count,
    up_translator,
    parent_to_child,
    receive_map,
):
    tile_x, tile_y = box_count.shape
    unknowns = currents.shape[-1]
    samples = low_translator.shape[-1]
    parent_samples = up_translator.shape[-1]
    kind_total = up_translator.shape[0]
    low_flat = low_translator.reshape(low_translator.shape[0], 2 * samples)
    mask = jnp.arange(unknowns, dtype=jnp.int32)[None, None, :] < box_count[:, :, None]
    live = jnp.where(mask[:, :, None, :], currents, jnp.zeros_like(currents))
    near_pad = extended(live, (("gx", 0), ("gy", 1)), 1)
    pattern = make_patterns(live, aggregate)
    pattern_pad = extended(pattern, (("gx", 0), ("gy", 1)), 2)
    lower_in = jnp.zeros((tile_x, tile_y, 2 * samples), jnp.float32)
    offset = 0
    for shift_x in range(-2, 3):
        for shift_y in range(-2, 3):
            if max(abs(shift_x), abs(shift_y)) < 2:
                continue
            source = pattern_pad[
                2 + shift_x : 2 + shift_x + tile_x, 2 + shift_y : 2 + shift_y + tile_y
            ]
            lower_in = lower_in + complex_flat(low_flat[offset], source, samples)
            offset += 1
    parents_x, parents_y = (tile_x // 2, tile_y // 2)
    children = pattern.reshape(parents_x, 2, parents_y, 2, 2 * samples)
    coarse_sum = jnp.zeros((parents_x * parents_y, 2 * parent_samples), jnp.float32)
    for half_x in range(2):
        for half_y in range(2):
            child = children[:, half_x, :, half_y].reshape(parents_x * parents_y, 2 * samples)
            coarse_sum = coarse_sum + jnp.dot(
                child, child_to_parent[2 * half_x + half_y], preferred_element_type=jnp.float32
            )
    coarse = coarse_sum.astype(jnp.bfloat16).reshape(parents_x, parents_y, 2 * parent_samples)
    group = lax.all_gather(coarse, "gy", axis=1, tiled=True)
    flat_group = group.reshape(group.shape[0] * group.shape[1], 2 * parent_samples)
    table = up_translator.reshape(kind_total, 2 * parent_samples)
    coarse_in = translate_group(flat_group, coarse_list, coarse_kind, coarse_count, table)
    coarse_flat = coarse_in.reshape(parents_x * parents_y, 2 * parent_samples)
    pieces = [
        jnp.dot(coarse_flat, parent_to_child[child_id], preferred_element_type=jnp.float32).reshape(
            parents_x, parents_y, 2 * samples
        )
        for child_id in range(4)
    ]
    rows_first = jnp.stack([pieces[0], pieces[1]], axis=2)
    rows_second = jnp.stack([pieces[2], pieces[3]], axis=2)
    from_parent = jnp.stack([rows_first, rows_second], axis=1).reshape(tile_x, tile_y, 2 * samples)
    incoming = (lower_in + from_parent).astype(jnp.bfloat16)
    field = jnp.dot(
        incoming.reshape(tile_x * tile_y, 2 * samples),
        receive_map,
        preferred_element_type=jnp.float32,
    )
    for shift_x in range(-1, 2):
        for shift_y in range(-1, 2):
            source = near_pad[
                1 + shift_x : 1 + shift_x + tile_x, 1 + shift_y : 1 + shift_y + tile_y
            ].reshape(tile_x * tile_y, 2 * unknowns)
            field = field + jnp.dot(
                source,
                near_blocks[3 * (shift_x + 1) + shift_y + 1],
                preferred_element_type=jnp.float32,
            )
    return field.reshape(tile_x, tile_y, 2, unknowns) * mask[:, :, None, :].astype(jnp.float32)


def solution(mesh):
    in_specs = (
        P("gx", "gy", None, None),
        P("gx", "gy"),
        P(),
        P(),
        P(),
        P(),
        P("gx", "gy", None),
        P("gx", "gy", None),
        P("gx", "gy"),
        P(),
        P(),
        P(),
    )
    out_specs = P("gx", "gy", None, None)
    return jax.shard_map(body, mesh=mesh, in_specs=in_specs, out_specs=out_specs, check_vma=False)
```

profile of v0, /device:TPU:8, one launch (start us, length us, event | category | flops | bytes accessed | tf_op | source)
XLA Modules:
  0.0 233.4 jit_solution(2320973562088822764)
XLA Ops:
  6.5 1.7 fusion.114
  8.3 1.9 broadcast_select_fusion.1
  10.7 1.1 fusion.119
  12.0 1.1 copy-done.13
  13.8 1.0 fusion.7
  14.8 1.7 collective-permute-start
  16.6 1.3 collective-permute-start.1
  17.9 5.2 %collective-permute-start.4 = (bf16[1,32,2,128]{3,2,1,0:T(2,128)(2,1)S(1)}, bf16[1,32,2,128]{3,2,1,0:T(2,128)(2,1)S(1)}, u32[]{:S(2)}, u32[]{:S(2)}) collective-permute-start(bf16[1,32,2,128]{3,2,1,0:T(2,128)(2,1)S(1)} %get-tuple-element.260), channel_id=1, source_target_pairs={{0,16},{16,32},{32,48},{48,64},{64,80},{80,96},{96,112},{112,128},... | collective-permute-start | bytes 49160 | tf_op jit(solution)/shard_map/ppermute | solution.py:15
  23.1 1.3 collective-permute-start.5
  24.8 2.7 %collective-permute-done.5 = bf16[1,32,2,128]{3,2,1,0:T(2,128)(2,1)S(1)} collective-permute-done((bf16[1,32,2,128]{3,2,1,0:T(2,128)(2,1)S(1)}, bf16[1,32,2,128]{3,2,1,0:T(2,128)(2,1)S(1)}, u32[]{:S(2)}, u32[]{:S(2)}) %collective-permute-start.5) | collective-permute-done | bytes 16416 | tf_op jit(solution)/shard_map/ppermute | solution.py:17
  27.5 4.9 %collective-permute-start.6 = (bf16[34,1,2,128]{3,2,1,0:T(2,128)(2,1)S(1)}, bf16[34,1,2,128]{3,2,1,0:T(2,128)(2,1)S(1)}, u32[]{:S(2)}, u32[]{:S(2)}) collective-permute-start(bf16[34,1,2,128]{3,2,1,0:T(2,128)(2,1)S(1)} %get-tuple-element.257), channel_id=1, source_target_pairs={{0,1},{1,2},{2,3},{3,4},{4,5},{5,6},{6,7},{7,8},{8,9},{9,10},{10,1... | collective-permute-start | bytes 52232 | tf_op jit(solution)/shard_map/ppermute | solution.py:15
  32.4 3.3 %collective-permute-start.7 = (bf16[34,1,2,128]{3,2,1,0:T(2,128)(2,1)S(1)}, bf16[34,1,2,128]{3,2,1,0:T(2,128)(2,1)S(1)}, u32[]{:S(2)}, u32[]{:S(2)}) collective-permute-start(bf16[34,1,2,128]{3,2,1,0:T(2,128)(2,1)S(1)} %get-tuple-element.256), channel_id=1, source_target_pairs={{1,0},{2,1},{3,2},{4,3},{5,4},{6,5},{7,6},{8,7},{9,8},{10,9},{11,1... | collective-permute-start | bytes 52232 | tf_op jit(solution)/shard_map/ppermute | solution.py:17
  35.8 2.4 %pad_maximum_fusion.3 = (bf16[32,32,2,128]{3,2,1,0:T(2,128)(2,1)}, bf16[32,32,2,128]{3,2,1,0:T(2,128)(2,1)}) fusion(bf16[1,32,2,128]{3,2,1,0:T(2,128)(2,1)S(1)} %collective-permute-done.5, bf16[32,32,2,128]{3,2,1,0:T(2,128)(2,1)S(1)} %broadcast_select_fusion.1, bf16[1,32,2,128]{3,2,1,0:T(2,128)(2,1)S(1)} %collective-permute-done.4), kind=kLoop, calls=%fused_computation.176 | loop fusion | flops 524288 | bytes 1605632 | tf_op jit(solution)/shard_map/concatenate | solution.py:13
  38.2 4.0 %collective-permute-start.2 = (bf16[36,2,256]{2,1,0:T(2,128)(2,1)S(1)}, bf16[36,2,256]{2,1,0:T(2,128)(2,1)S(1)}, u32[]{:S(2)}, u32[]{:S(2)}) collective-permute-start(bf16[36,2,256]{2,1,0:T(2,128)(2,1)S(1)} %get-tuple-element.242), channel_id=1, source_target_pairs={{0,1},{1,2},{2,3},{3,4},{4,5},{5,6},{6,7},{7,8},{8,9},{9,10},{10,1... | collective-permute-start | bytes 110600 | tf_op jit(solution)/shard_map/ppermute | solution.py:15
  42.3 4.4 %collective-permute-start.3 = (bf16[36,2,256]{2,1,0:T(2,128)(2,1)S(1)}, bf16[36,2,256]{2,1,0:T(2,128)(2,1)S(1)}, u32[]{:S(2)}, u32[]{:S(2)}) collective-permute-start(bf16[36,2,256]{2,1,0:T(2,128)(2,1)S(1)} %get-tuple-element.243), channel_id=1, source_target_pairs={{1,0},{2,1},{3,2},{4,3},{5,4},{6,5},{7,6},{8,7},{9,8},{10,9},{11,1... | collective-permute-start | bytes 110600 | tf_op jit(solution)/shard_map/ppermute | solution.py:17
  46.7 1.1 fusion.50
  47.8 1.1 fusion.28
  48.9 2.1 pad_maximum_fusion.2
  51.1 4.4 %fusion.115 = (bf16[32,32,2,128]{3,2,1,0:T(2,128)(2,1)}, bf16[32,32,2,128]{3,2,1,0:T(2,128)(2,1)}, bf16[32,32,2,128]{3,2,1,0:T(2,128)(2,1)}, bf16[32,32,2,128]{3...) fusion(bf16[34,33,2,128]{3,2,1,0:T(2,128)(2,1)S(1)} %get-tuple-element.254, ...), kind=kLoop, calls=%fused_computation.264 | loop fusion | bytes 6291456 | tf_op jit(solution)/shard_map/slice | solution.py:131
  56.0 1.7 fusion.34
  57.7 2.1 fusion.24
  59.8 2.1 fusion.26
  62.0 2.5 %fusion.32 = (f32[32,32,128]{2,1,0:T(8,128)}, f32[32,32,128]{2,1,0:T(8,128)}, f32[32,32,128]{2,1,0:T(8,128)}, f32[32,32,128]{2,1,0:T(8,128)}, f32[32,32,128]{2,1,0:T(8,128)}, /*index=5*/f32[32,32,128]{2,1,0:T(8,128)}) fusion(f32[128]{0:T(128)S(1)} %get-tuple-element.292, f32[128]{0:T(128)S(1)} %get-tuple-element.293, ...), kind=kLoop, calls=%fused_computation.134 | loop fusion | flops 3145728 | bytes 4721664 | tf_op jit(solution)/shard_map/sub | solution.py:27
  64.4 2.4 %fusion.30 = (f32[32,32,128]{2,1,0:T(8,128)}, f32[32,32,128]{2,1,0:T(8,128)}, f32[32,32,128]{2,1,0:T(8,128)}, f32[32,32,128]{2,1,0:T(8,128)}, f32[32,32,128]{2,1,0:T(8,128)}, /*index=5*/f32[32,32,128]{2,1,0:T(8,128)}) fusion(f32[128]{0:T(128)S(1)} %get-tuple-element.294, f32[128]{0:T(128)S(1)} %get-tuple-element.295, ...), kind=kLoop, calls=%fused_computation.132 | loop fusion | flops 3145728 | bytes 4721664 | tf_op jit(solution)/shard_map/sub | solution.py:27
  66.8 58.1 %all-gather.2.cloned.1.call-done = bf16[16,256,512]{2,1,0:T(8,128)(2,1)} async-done(((bf16[16,16,512]{2,1,0:T(8,128)(2,1)}), bf16[16,256,512]{2,1,0:T(8,128)(2,1)}) %all-gather.2.cloned.1.call-update) | async-done | bytes 4194320 | tf_op jit(solution)/shard_map/all_gather | solution.py:109
  125.0 81.5 %while.14 = (s32[]{:T(128)}, f32[256,512]{1,0:T(8,128)S(1)}, s32[16,16]{1,0:T(8,128)S(1)}, s32[16,16,16]{1,0,2:T(8,128)S(1)}, f32[64,512]{1,0:T(8,128)S(1)}, /*i...) while((s32[]{:T(128)}, f32[256,512]{1,0:T(8,128)S(1)}, ...), condition=%wide.region_1.2_spmd.clone, body=%wide.region_0.1_spmd.clone.sunk | while | flops 101862912 | bytes 4610671 | solution.py:59
  125.1 4.0 %gather_fusion = bf16[256,512]{1,0:T(8,128)(2,1)S(1)} fusion(bf16[4096,512]{1,0:T(8,128)(2,1)} %get-tuple-element.384, s32[1024]{0:T(1024)S(1)} %pad_clamp_fusion.2), kind=kCustom, calls=%fused_computation.clone.clone.1 | custom fusion | bytes 525312 | tf_op jit(solution)/shard_map/while/body/eval_jaxpr/jit(_take)/gather | solution.py:47
  130.2 3.9 %gather_fusion = bf16[256,512]{1,0:T(8,128)(2,1)S(1)} fusion(bf16[4096,512]{1,0:T(8,128)(2,1)} %get-tuple-element.384, s32[1024]{0:T(1024)S(1)} %pad_clamp_fusion.2), kind=kCustom, calls=%fused_computation.clone.clone.1 | custom fusion | bytes 525312 | tf_op jit(solution)/shard_map/while/body/eval_jaxpr/jit(_take)/gather | solution.py:47
  135.3 3.9 %gather_fusion = bf16[256,512]{1,0:T(8,128)(2,1)S(1)} fusion(bf16[4096,512]{1,0:T(8,128)(2,1)} %get-tuple-element.384, s32[1024]{0:T(1024)S(1)} %pad_clamp_fusion.2), kind=kCustom, calls=%fused_computation.clone.clone.1 | custom fusion | bytes 525312 | tf_op jit(solution)/shard_map/while/body/eval_jaxpr/jit(_take)/gather | solution.py:47
  140.4 3.9 %gather_fusion = bf16[256,512]{1,0:T(8,128)(2,1)S(1)} fusion(bf16[4096,512]{1,0:T(8,128)(2,1)} %get-tuple-element.384, s32[1024]{0:T(1024)S(1)} %pad_clamp_fusion.2), kind=kCustom, calls=%fused_computation.clone.clone.1 | custom fusion | bytes 525312 | tf_op jit(solution)/shard_map/while/body/eval_jaxpr/jit(_take)/gather | solution.py:47
  145.5 3.9 %gather_fusion = bf16[256,512]{1,0:T(8,128)(2,1)S(1)} fusion(bf16[4096,512]{1,0:T(8,128)(2,1)} %get-tuple-element.384, s32[1024]{0:T(1024)S(1)} %pad_clamp_fusion.2), kind=kCustom, calls=%fused_computation.clone.clone.1 | custom fusion | bytes 525312 | tf_op jit(solution)/shard_map/while/body/eval_jaxpr/jit(_take)/gather | solution.py:47
  150.6 3.9 %gather_fusion = bf16[256,512]{1,0:T(8,128)(2,1)S(1)} fusion(bf16[4096,512]{1,0:T(8,128)(2,1)} %get-tuple-element.384, s32[1024]{0:T(1024)S(1)} %pad_clamp_fusion.2), kind=kCustom, calls=%fused_computation.clone.clone.1 | custom fusion | bytes 525312 | tf_op jit(solution)/shard_map/while/body/eval_jaxpr/jit(_take)/gather | solution.py:47
  155.7 3.9 %gather_fusion = bf16[256,512]{1,0:T(8,128)(2,1)S(1)} fusion(bf16[4096,512]{1,0:T(8,128)(2,1)} %get-tuple-element.384, s32[1024]{0:T(1024)S(1)} %pad_clamp_fusion.2), kind=kCustom, calls=%fused_computation.clone.clone.1 | custom fusion | bytes 525312 | tf_op jit(solution)/shard_map/while/body/eval_jaxpr/jit(_take)/gather | solution.py:47
  160.8 3.9 %gather_fusion = bf16[256,512]{1,0:T(8,128)(2,1)S(1)} fusion(bf16[4096,512]{1,0:T(8,128)(2,1)} %get-tuple-element.384, s32[1024]{0:T(1024)S(1)} %pad_clamp_fusion.2), kind=kCustom, calls=%fused_computation.clone.clone.1 | custom fusion | bytes 525312 | tf_op jit(solution)/shard_map/while/body/eval_jaxpr/jit(_take)/gather | solution.py:47
  165.9 3.9 %gather_fusion = bf16[256,512]{1,0:T(8,128)(2,1)S(1)} fusion(bf16[4096,512]{1,0:T(8,128)(2,1)} %get-tuple-element.384, s32[1024]{0:T(1024)S(1)} %pad_clamp_fusion.2), kind=kCustom, calls=%fused_computation.clone.clone.1 | custom fusion | bytes 525312 | tf_op jit(solution)/shard_map/while/body/eval_jaxpr/jit(_take)/gather | solution.py:47
  171.0 3.9 %gather_fusion = bf16[256,512]{1,0:T(8,128)(2,1)S(1)} fusion(bf16[4096,512]{1,0:T(8,128)(2,1)} %get-tuple-element.384, s32[1024]{0:T(1024)S(1)} %pad_clamp_fusion.2), kind=kCustom, calls=%fused_computation.clone.clone.1 | custom fusion | bytes 525312 | tf_op jit(solution)/shard_map/while/body/eval_jaxpr/jit(_take)/gather | solution.py:47
  176.1 3.9 %gather_fusion = bf16[256,512]{1,0:T(8,128)(2,1)S(1)} fusion(bf16[4096,512]{1,0:T(8,128)(2,1)} %get-tuple-element.384, s32[1024]{0:T(1024)S(1)} %pad_clamp_fusion.2), kind=kCustom, calls=%fused_computation.clone.clone.1 | custom fusion | bytes 525312 | tf_op jit(solution)/shard_map/while/body/eval_jaxpr/jit(_take)/gather | solution.py:47
  181.1 3.9 %gather_fusion = bf16[256,512]{1,0:T(8,128)(2,1)S(1)} fusion(bf16[4096,512]{1,0:T(8,128)(2,1)} %get-tuple-element.384, s32[1024]{0:T(1024)S(1)} %pad_clamp_fusion.2), kind=kCustom, calls=%fused_computation.clone.clone.1 | custom fusion | bytes 525312 | tf_op jit(solution)/shard_map/while/body/eval_jaxpr/jit(_take)/gather | solution.py:47
  186.2 3.9 %gather_fusion = bf16[256,512]{1,0:T(8,128)(2,1)S(1)} fusion(bf16[4096,512]{1,0:T(8,128)(2,1)} %get-tuple-element.384, s32[1024]{0:T(1024)S(1)} %pad_clamp_fusion.2), kind=kCustom, calls=%fused_computation.clone.clone.1 | custom fusion | bytes 525312 | tf_op jit(solution)/shard_map/while/body/eval_jaxpr/jit(_take)/gather | solution.py:47
  191.3 3.9 %gather_fusion = bf16[256,512]{1,0:T(8,128)(2,1)S(1)} fusion(bf16[4096,512]{1,0:T(8,128)(2,1)} %get-tuple-element.384, s32[1024]{0:T(1024)S(1)} %pad_clamp_fusion.2), kind=kCustom, calls=%fused_computation.clone.clone.1 | custom fusion | bytes 525312 | tf_op jit(solution)/shard_map/while/body/eval_jaxpr/jit(_take)/gather | solution.py:47
  196.4 3.9 %gather_fusion = bf16[256,512]{1,0:T(8,128)(2,1)S(1)} fusion(bf16[4096,512]{1,0:T(8,128)(2,1)} %get-tuple-element.384, s32[1024]{0:T(1024)S(1)} %pad_clamp_fusion.2), kind=kCustom, calls=%fused_computation.clone.clone.1 | custom fusion | bytes 525312 | tf_op jit(solution)/shard_map/while/body/eval_jaxpr/jit(_take)/gather | solution.py:47
  201.5 3.9 %gather_fusion = bf16[256,512]{1,0:T(8,128)(2,1)S(1)} fusion(bf16[4096,512]{1,0:T(8,128)(2,1)} %get-tuple-element.384, s32[1024]{0:T(1024)S(1)} %pad_clamp_fusion.2), kind=kCustom, calls=%fused_computation.clone.clone.1 | custom fusion | bytes 525312 | tf_op jit(solution)/shard_map/while/body/eval_jaxpr/jit(_take)/gather | solution.py:47
  207.6 0.8 copy.19
  209.5 6.5 %fusion.74 = f32[1024,256]{1,0:T(8,128)S(1)} fusion(bf16[256,256]{1,0:T(8,128)(2,1)S(1)} %copy-done.15, f32[1024,256]{1,0:T(8,128)S(1)} %reshape.262, f32[1024,128]{1,0:T(8,128)} %bitcast.276, f32[1024,128]{1,0:T(8,128)} %bitcast.277, f32[1024,128]{1,0:T(8,128)} %bitcast.278, f32[1024,128]{1,0:T(8,128)} %bitcast.279, f32[1024,128]{1,0:T(8,128)} %bitcast.289, ...), kind=kOutput, calls=%fused_computation.182 | convolution fusion | flops 142868480 | bytes 19005440 | tf_op jit(solution)/shard_map/dot_general | solution.py:124
  218.5 0.7 copy-done.8
  220.9 0.7 copy-done.6
  221.9 0.7 copy-done.3
  225.0 1.5 broadcast_multiply_fusion
  (291 shorter events, 28.4 us)
Async XLA Ops:
  6.5 3.7 %copy-start = (bf16[256,256]{1,0:T(8,128)(2,1)S(1)}, bf16[256,256]{1,0:T(8,128)(2,1)}, u32[]{:S(2)}) copy-start(bf16[256,256]{1,0:T(8,128)(2,1)} %param.16) | copy-start | bytes 393220
  6.5 118.4 %all-gather.2.cloned.1.call-start = ((), (), s32[]{:S(2)}) async-start(), calls=%async_computation | async-start | bytes 4456448 | tf_op jit(solution)/shard_map/all_gather | solution.py:109
  11.9 1.2 copy-start.13
  13.8 10.6 %copy-start.19 = (f32[16,2,128]{2,1,0:T(2,128)S(1)}, f32[16,2,128]{2,1,0:T(2,128)}, u32[]{:S(2)}) copy-start(f32[16,2,128]{2,1,0:T(2,128)} %param.18) | copy-start | bytes 49156
  13.8 10.7 %copy-start.16 = (f32[64,2,256]{2,1,0:T(2,128)S(1)}, f32[64,2,256]{2,1,0:T(2,128)}, u32[]{:S(2)}) copy-start(f32[64,2,256]{2,1,0:T(2,128)} %param.23) | copy-start | bytes 393220
  13.8 10.7 %copy-start.17 = (s32[16,16,16]{2,1,0:T(8,128)S(1)}, s32[16,16,16]{2,1,0:T(8,128)}, u32[]{:S(2)}) copy-start(s32[16,16,16]{2,1,0:T(8,128)} %param.21) | copy-start | bytes 49156
  13.8 10.8 %copy-start.18 = (s32[16,16,16]{2,1,0:T(8,128)S(1)}, s32[16,16,16]{2,1,0:T(8,128)}, u32[]{:S(2)}) copy-start(s32[16,16,16]{2,1,0:T(8,128)} %param.20) | copy-start | bytes 49156
  14.8 23.3 %collective-permute-start = (bf16[2,32,256]{2,1,0:T(8,128)(2,1)S(1)}, bf16[2,32,256]{2,1,0:T(8,128)(2,1)S(1)}, u32[]{:S(2)}, u32[]{:S(2)}) collective-permute-start(bf16[2,32,256]{2,1,0:T(8,128)(2,1)S(1)} %bitcast.304), channel_id=1, source_target_pairs={{0,16},{16,32},{32,48},{48,64},{64,80},{80,96},{96,112},{112,128},... | collective-permute-start | bytes 98312 | tf_op jit(solution)/shard_map/ppermute | solution.py:15
  16.6 21.6 %collective-permute-start.1 = (bf16[2,32,256]{2,1,0:T(8,128)(2,1)S(1)}, bf16[2,32,256]{2,1,0:T(8,128)(2,1)S(1)}, u32[]{:S(2)}, u32[]{:S(2)}) collective-permute-start(bf16[2,32,256]{2,1,0:T(8,128)(2,1)S(1)} %bitcast.303), channel_id=1, source_target_pairs={{16,0},{32,16},{48,32},{64,48},{80,64},{96,80},{112,96},{128,112},... | collective-permute-start | bytes 98312 | tf_op jit(solution)/shard_map/ppermute | solution.py:17
  17.9 6.8 %collective-permute-start.4 = (bf16[1,32,2,128]{3,2,1,0:T(2,128)(2,1)S(1)}, bf16[1,32,2,128]{3,2,1,0:T(2,128)(2,1)S(1)}, u32[]{:S(2)}, u32[]{:S(2)}) collective-permute-start(bf16[1,32,2,128]{3,2,1,0:T(2,128)(2,1)S(1)} %get-tuple-element.260), channel_id=1, source_target_pairs={{0,16},{16,32},{32,48},{48,64},{64,80},{80,96},{96,112},{112,128},... | collective-permute-start | bytes 49160 | tf_op jit(solution)/shard_map/ppermute | solution.py:15
  23.1 4.3 %collective-permute-start.5 = (bf16[1,32,2,128]{3,2,1,0:T(2,128)(2,1)S(1)}, bf16[1,32,2,128]{3,2,1,0:T(2,128)(2,1)S(1)}, u32[]{:S(2)}, u32[]{:S(2)}) collective-permute-start(bf16[1,32,2,128]{3,2,1,0:T(2,128)(2,1)S(1)} %get-tuple-element.261), channel_id=1, source_target_pairs={{16,0},{32,16},{48,32},{64,48},{80,64},{96,80},{112,96},{128,112},... | collective-permute-start | bytes 49160 | tf_op jit(solution)/shard_map/ppermute | solution.py:17
  27.5 21.5 %collective-permute-start.6 = (bf16[34,1,2,128]{3,2,1,0:T(2,128)(2,1)S(1)}, bf16[34,1,2,128]{3,2,1,0:T(2,128)(2,1)S(1)}, u32[]{:S(2)}, u32[]{:S(2)}) collective-permute-start(bf16[34,1,2,128]{3,2,1,0:T(2,128)(2,1)S(1)} %get-tuple-element.257), channel_id=1, source_target_pairs={{0,1},{1,2},{2,3},{3,4},{4,5},{5,6},{6,7},{7,8},{8,9},{9,10},{10,1... | collective-permute-start | bytes 52232 | tf_op jit(solution)/shard_map/ppermute | solution.py:15
  32.4 16.5 %collective-permute-start.7 = (bf16[34,1,2,128]{3,2,1,0:T(2,128)(2,1)S(1)}, bf16[34,1,2,128]{3,2,1,0:T(2,128)(2,1)S(1)}, u32[]{:S(2)}, u32[]{:S(2)}) collective-permute-start(bf16[34,1,2,128]{3,2,1,0:T(2,128)(2,1)S(1)} %get-tuple-element.256), channel_id=1, source_target_pairs={{1,0},{2,1},{3,2},{4,3},{5,4},{6,5},{7,6},{8,7},{9,8},{10,9},{11,1... | collective-permute-start | bytes 52232 | tf_op jit(solution)/shard_map/ppermute | solution.py:17
  38.2 17.3 %collective-permute-start.2 = (bf16[36,2,256]{2,1,0:T(2,128)(2,1)S(1)}, bf16[36,2,256]{2,1,0:T(2,128)(2,1)S(1)}, u32[]{:S(2)}, u32[]{:S(2)}) collective-permute-start(bf16[36,2,256]{2,1,0:T(2,128)(2,1)S(1)} %get-tuple-element.242), channel_id=1, source_target_pairs={{0,1},{1,2},{2,3},{3,4},{4,5},{5,6},{6,7},{7,8},{8,9},{9,10},{10,1... | collective-permute-start | bytes 110600 | tf_op jit(solution)/shard_map/ppermute | solution.py:15
  42.3 13.2 %collective-permute-start.3 = (bf16[36,2,256]{2,1,0:T(2,128)(2,1)S(1)}, bf16[36,2,256]{2,1,0:T(2,128)(2,1)S(1)}, u32[]{:S(2)}, u32[]{:S(2)}) collective-permute-start(bf16[36,2,256]{2,1,0:T(2,128)(2,1)S(1)} %get-tuple-element.243), channel_id=1, source_target_pairs={{1,0},{2,1},{3,2},{4,3},{5,4},{6,5},{7,6},{8,7},{9,8},{10,9},{11,1... | collective-permute-start | bytes 110600 | tf_op jit(solution)/shard_map/ppermute | solution.py:17
  64.4 60.5 %copy-start.14 = (s32[16,16]{1,0:T(8,128)S(1)}, s32[16,16]{1,0:T(8,128)}, u32[]{:S(2)}) copy-start(s32[16,16]{1,0:T(8,128)} %param.22) | copy-start | bytes 3076
  125.0 81.6 %copy-start.12 = (bf16[4,512,256]{2,1,0:T(8,128)(2,1)S(1)}, bf16[4,512,256]{2,1,0:T(8,128)(2,1)}, u32[]{:S(2)}) copy-start(bf16[4,512,256]{2,1,0:T(8,128)(2,1)} %param.24) | copy-start | bytes 3145732
  208.5 1.0 copy-start.1
  208.5 1.1 copy-start.15
  209.5 6.5 %copy-start.10 = (bf16[32,32,2,128]{3,2,1,0:T(2,128)(2,1)S(1)}, bf16[32,32,2,128]{3,2,1,0:T(2,128)(2,1)}, u32[]{:S(2)}) copy-start(bf16[32,32,2,128]{3,2,1,0:T(2,128)(2,1)} %get-tuple-element.302) | copy-start | bytes 1572868
  209.5 6.5 %copy-start.11 = (bf16[9,256,256]{2,1,0:T(8,128)(2,1)S(1)}, bf16[9,256,256]{2,1,0:T(8,128)(2,1)}, u32[]{:S(2)}) copy-start(bf16[9,256,256]{2,1,0:T(8,128)(2,1)} %param.17) | copy-start | bytes 3538948
  216.1 1.0 copy-start.4
  217.1 1.0 copy-start.9
  218.2 1.0 copy-start.8
  219.5 1.0 copy-start.7
  220.6 1.0 copy-start.6
  221.6 1.0 copy-start.3
  222.7 1.0 copy-start.5
  224.0 1.0 copy-start.2
Sparse Core Ops, SparseCore 0:
  14.9 109.9 all-gather.1
where the time goes:
time: 235 us; the launch traced here: 233 us
  local copies, waits for them, and re-layouts  83.8 us (36%)
  waiting for transfers between devices  60.8 us (26%)
  other arithmetic  29.2 us (12%)
  starting transfers between devices  26.2 us (11%)
  matrix products  18.6 us (8%)
  between operations  13.9 us (6%)
    gather x16, local copies, waits for them, and re-layouts, accumulate(): source = jnp.take(flat_group, index, axis=0)  63.1 us
    all_gather x1, waiting for transfers between devices, body(): group = lax.all_gather(coarse, 'gy', axis=1, tiled=True)  58.1 us
    ppermute x4, starting transfers between devices, extended(): lax.ppermute(tail, axis, [(i, (i + 1) % count) for i in range(ends)])  15.9 us
    sub x23, other arithmetic, complex_flat(): first = table[..., :half] * real_part - table[..., half:] * imag_part  14.4 us
    ppermute x4, starting transfers between devices, extended(): lax.ppermute(head, axis, [((i + 1) % count, i) for i in range(ends)])  10.3 us
    unnamed x47, local copies, waits for them, and re-layouts  7.43 us
    dot_general x16, matrix products, accumulate(): jnp.dot(choose, table, precision=lax.Precision.HIGHEST, preferred_element...  6.53 us
    dot_general x1, matrix products, body(): jnp.dot(incoming.reshape(tile_x * tile_y, 2 * samples), receive_map, pref...  6.53 us
  transfers between devices with their start and end apart: 9, of which 2 were waited for; matrix products, arithmetic and copies ran while one was open for 10% of the time, Pallas kernels for 0%

commit v1 on v0

v1 whole, which is shorter than its diff:
```python
import functools

import jax
import jax.numpy as jnp
from jax import lax
from jax.experimental import pallas as pl
from jax.experimental.pallas import tpu as pltpu
from jax.sharding import PartitionSpec as P

F32 = jnp.float32
BF16 = jnp.bfloat16
MESH = pl.DeviceIdType.MESH
TX = 32
TY = 32
PITCH = 80
WIDE = TX + 4
ROWS = 1024
FIRST = 448
OFFSETS = [(dx, dy) for dx in range(-2, 3) for dy in range(-2, 3) if max(abs(dx), abs(dy)) == 2]


def remote(src, dst, send, recv, device):
    return pltpu.make_async_remote_copy(
        src_ref=src, dst_ref=dst, send_sem=send, recv_sem=recv, device_id=device, device_id_type=MESH
    )


def gather_kernel(
    n_gx,
    n_gy,
    cur,
    cnt,
    agg,
    near,
    low,
    c2p,
    group,
    lower_out,
    near_out,
    mask_out,
    sel_rows,
    cntb,
    lf,
    pf,
    ll,
    pv,
    cf,
    own,
    s_lo,
    s_hi,
    h_lo,
    h_hi,
    low_v,
    near_v,
    ys,
    yr,
    xs,
    xr,
    hs,
    hr,
    loc,
):
    gx = lax.axis_index("gx")
    gy = lax.axis_index("gy")
    ring = n_gy // 2
    y = gy // 2
    xh = lax.rem(gy, 2)
    px = 1 - xh

    def slot(yy, xx):
        return lax.rem(yy + ring, ring) * 2 + xx

    x_next = {"gx": lax.rem(gx + 1, n_gx)}
    x_prev = {"gx": lax.rem(gx + n_gx - 1, n_gx)}
    y_next = {"gy": lax.rem(gy + 1, n_gy)}
    y_prev = {"gy": lax.rem(gy + n_gy - 1, n_gy)}
    r_next = {"gy": slot(y + 1, xh)}
    r_prev = {"gy": slot(y - 1, xh)}
    r_cross = {"gy": slot(y, px)}
    barrier = pltpu.get_barrier_semaphore()
    for device in (x_next, x_prev, y_next, y_prev, r_next, r_prev):
        pl.semaphore_signal(barrier, inc=1, device_id=device, device_id_type=MESH)

    pick = (
        lax.broadcasted_iota(jnp.int32, (2 * TY, TY), 0) // 2 == lax.broadcasted_iota(jnp.int32, (2 * TY, TY), 1)
    ).astype(F32)
    for i in range(TX):
        line = jnp.broadcast_to(cnt[pl.ds(i, 1), :].astype(F32), (2 * TY, TY))
        sel_rows[pl.ds(2 * TY * i, 2 * TY), :] = (line * pick).astype(BF16)
    cntb[...] = jnp.dot(sel_rows[...], jnp.ones((TY, 128), BF16), preferred_element_type=F32)
    lane = lax.broadcasted_iota(jnp.int32, (2 * TY, 128), 1).astype(F32)
    for i in range(TX):
        rows = pl.ds(2 * TY * i, 2 * TY)
        live = jnp.where(lane < cntb[rows, :], cur[rows, :].astype(F32), 0.0)
        lf[pl.ds(PITCH * (i + 2) + 8, 2 * TY), :] = live

    def piece(ref, x, start):
        real = ref[pl.ds(PITCH * x + start, 16, stride=4), :]
        imag = ref[pl.ds(PITCH * x + start + 1, 16, stride=4), :]
        return real, imag

    def plane(x, k):
        real, imag = piece(lf, x, 6 + 2 * k)
        base = 64 * x + 16 * k
        ll[pl.ds(base, 16), :] = jnp.concatenate([real, imag], axis=1).astype(BF16)

    for i in range(TX):
        for k in (1, 2):
            plane(i + 2, k)

    def lines(ref, x, count, k, planes):
        parts = [ref[pl.ds(64 * (x + n) + 16 * k, 16 * planes), :] for n in range(count)]
        return jnp.concatenate(parts, axis=0)

    def spread(x, b, value):
        for h in range(2):
            pf[pl.ds(PITCH * x + 8 + 2 * b + h, 16, stride=4), :] = value[:, 128 * h : 128 * h + 128]

    for block in range(4):
        got = jnp.dot(lines(ll, 2 + 8 * block, 8, 1, 2), agg[...], preferred_element_type=F32).astype(BF16)
        pv[pl.ds(256 * block, 256), :] = got

    total = jnp.zeros((256, 512), F32)
    for q in range(4):
        child = jnp.concatenate([pv[pl.ds(64 * p + 16 * q, 16), :] for p in range(16)], axis=0)
        total = total + jnp.dot(child, c2p[pl.ds(256 * q, 256), :], preferred_element_type=F32)
    for q in range(4):
        cf[pl.ds(q, 256, stride=4), :] = total[:, 128 * q : 128 * q + 128]
    own[...] = cf[...].astype(BF16)

    pl.semaphore_wait(barrier, 6)

    sign = (1, -1)
    along = (r_next, r_prev)
    sent = []

    def go(copy):
        copy.start()
        sent.append(copy)

    def span(dr, d, w):
        n = ROWS if w == 0 else FIRST
        if d < 3:
            return 0, n
        return (0, n // 2) if dr == 0 else (n // 2, n - n // 2)

    def y_send(dr, d, w):
        start, n = span(dr, d, w)
        where = group.at[slot(y - sign[dr] * d, xh if w == 0 else px), pl.ds(start, n)]
        src = own.at[pl.ds(start, n)] if (d == 0 and w == 0) else where
        go(remote(src, where, ys.at[dr, d, w], yr.at[dr, d, w], along[dr]))

    def y_wait(dr, d, w):
        start, n = span(dr, d, w)
        where = group.at[slot(y - sign[dr] * (d + 1), xh if w == 0 else px), pl.ds(start, n)]
        remote(where, where, ys.at[dr, d, w], yr.at[dr, d, w], along[dr]).wait_recv()

    def x_send(k, yy, start, n, mine=False):
        where = group.at[slot(yy, xh), pl.ds(start, n)]
        src = own.at[pl.ds(start, n)] if mine else where
        go(remote(src, where, xs.at[k], xr.at[k], r_cross))

    def x_wait(k, yy, start, n):
        where = group.at[slot(yy, px), pl.ds(start, n)]
        remote(where, where, xs.at[k], xr.at[k], r_cross).wait_recv()

    x_send(0, y, 0, FIRST, True)
    y_send(0, 0, 0)
    y_send(1, 0, 0)
    x_send(1, y, FIRST, ROWS - FIRST, True)
    local = pltpu.make_async_copy(own, group.at[gy], loc.at[0])
    local.start()

    def x_halo(k):
        src = (2, 3, TX, TX + 1)[k]
        dst = (TX + 2, TX + 3, 0, 1)[k]
        return remote(
            lf.at[pl.ds(PITCH * src + 8, 2 * TY)],
            lf.at[pl.ds(PITCH * dst + 8, 2 * TY)],
            hs.at[k],
            hr.at[k],
            x_prev if k < 2 else x_next,
        )

    halo = [x_halo(k) for k in range(4)]
    for copy in halo:
        copy.start()

    own_lane = lax.broadcasted_iota(jnp.int32, (16, 128), 1).astype(F32)
    for i in range(TX):
        for b in range(2):
            held = cntb[pl.ds(64 * i + 2 * b, 16, stride=4), :]
            mask_out_rows = jnp.where(own_lane < held, 1.0, 0.0)
            cf_rows = pl.ds(32 * i + 16 * b, 16)
            low_v[cf_rows, pl.ds(0, 128)] = mask_out_rows
    mask_copy = pltpu.make_async_copy(low_v.at[:, pl.ds(0, 128)], mask_out, loc.at[1])
    mask_copy.start()
    for i in range(TX):
        for b in range(2):
            spread(i + 2, b, pv[pl.ds(32 * i + 16 * b, 16), :].astype(F32))

    for copy in halo:
        copy.wait()

    @pl.when(gx == 0)
    def _():
        for x in (0, 1):
            lf[pl.ds(PITCH * x + 8, 2 * TY), :] = jnp.zeros((2 * TY, 128), F32)

    @pl.when(gx == n_gx - 1)
    def _():
        for x in (TX + 2, TX + 3):
            lf[pl.ds(PITCH * x + 8, 2 * TY), :] = jnp.zeros((2 * TY, 128), F32)

    for x in range(0, WIDE, 2):
        for buf, start in ((s_lo, 8), (s_hi, 2 * TY)):
            pair = [lf[pl.ds(PITCH * (x + e) + start, 8), :] for e in range(2)]
            buf[pl.ds(8 * x, 16), :] = jnp.concatenate(pair, axis=0).astype(BF16)
    halo_y = [
        remote(s_lo, h_hi, hs.at[4], hr.at[4], y_prev),
        remote(s_hi, h_lo, hs.at[5], hr.at[5], y_next),
    ]
    for copy in halo_y:
        copy.start()

    x_wait(0, y, 0, FIRST)
    y_send(0, 0, 1)
    y_send(1, 0, 1)

    for x in (0, 1, TX + 2, TX + 3):
        for k in (1, 2):
            plane(x, k)
    for x in (0, TX + 2):
        got = jnp.dot(lines(ll, x, 2, 1, 2), agg[...], preferred_element_type=F32).astype(BF16).astype(F32)
        for e in range(2):
            for b in range(2):
                spread(x + e, b, got[32 * e + 16 * b : 32 * e + 16 * b + 16])

    for copy in halo_y:
        copy.wait()

    @pl.when(gy == 0)
    def _():
        h_lo[...] = jnp.zeros_like(h_lo)

    @pl.when(gy == n_gy - 1)
    def _():
        h_hi[...] = jnp.zeros_like(h_hi)

    for x in range(0, WIDE, 2):
        for buf, start in ((h_lo, 0), (h_hi, 2 * TY + 8)):
            pair = buf[pl.ds(8 * x, 16), :].astype(F32)
            for e in range(2):
                lf[pl.ds(PITCH * (x + e) + start, 8), :] = pair[8 * e : 8 * e + 8]

    for start in (4, 6, 2 * TY + 8, 2 * TY + 10):
        cols = [lf[pl.ds(start + h, WIDE, stride=PITCH), :] for h in range(2)]
        lhs = jnp.concatenate(cols, axis=1)
        lhs = jnp.concatenate([lhs, jnp.zeros((48 - WIDE, 256), F32)], axis=0).astype(BF16)
        got = jnp.dot(lhs, agg[...], preferred_element_type=F32).astype(BF16).astype(F32)
        for h in range(2):
            pf[pl.ds(start + h, WIDE, stride=PITCH), :] = got[:WIDE, 128 * h : 128 * h + 128]

    crossed = []

    def step(d, w, dr):
        y_wait(dr, d - 1, w)
        y_send(dr, d, w)
        if w == 0:
            k = 2 + (d - 1) * 2 + dr
            yy = y - sign[dr] * d
            x_send(k, yy, FIRST, ROWS - FIRST)
            crossed.append((k, yy))

    def near_chunk(c):
        acc = jnp.zeros((256, 256), F32)
        for dx in range(3):
            for dy in range(3):
                lhs = lines(ll, 8 * c + 1 + dx, 8, dy, 2)
                acc = acc + jnp.dot(lhs, near[pl.ds(256 * (3 * dx + dy), 256), :], preferred_element_type=F32)
        near_v[pl.ds(256 * c, 256), :] = acc

    def lower_line(i, _):
        for b in range(2):
            first = jnp.zeros((16, 128), F32)
            second = jnp.zeros((16, 128), F32)
            for k, (dx, dy) in enumerate(OFFSETS):
                base = PITCH * (i + 2 + dx) + 8 + 2 * b + 2 * dy
                real = pf[pl.ds(base, 16, stride=4), :]
                imag = pf[pl.ds(base + 1, 16, stride=4), :]
                t0 = low[pl.ds(2 * k, 1), :]
                t1 = low[pl.ds(2 * k + 1, 1), :]
                first = first + (t0 * real - t1 * imag)
                second = second + (t0 * imag + t1 * real)
            rows = pl.ds(pl.multiple_of(32 * i + 16 * b, 16), 16)
            low_v[rows, pl.ds(0, 128)] = first
            low_v[rows, pl.ds(128, 128)] = second
        return 0

    step(1, 0, 0)
    step(1, 0, 1)
    for x in range(1, WIDE - 1):
        for k in (0, 3):
            plane(x, k)
    step(1, 1, 0)
    step(1, 1, 1)
    near_chunk(0)
    near_chunk(1)
    step(2, 0, 0)
    step(2, 0, 1)
    near_chunk(2)
    near_chunk(3)
    near_copy = pltpu.make_async_copy(near_v, near_out, loc.at[2])
    near_copy.start()
    mask_copy.wait()
    step(2, 1, 0)
    step(2, 1, 1)
    lax.fori_loop(0, TX // 2, lower_line, 0)
    step(3, 0, 0)
    step(3, 0, 1)
    lax.fori_loop(TX // 2, TX, lower_line, 0)
    low_copy = pltpu.make_async_copy(low_v, lower_out, loc.at[3])
    low_copy.start()
    step(3, 1, 0)
    step(3, 1, 1)
    y_wait(0, 3, 0)
    y_wait(1, 3, 0)
    x_send(8, y - 4, FIRST, ROWS - FIRST)
    crossed.append((8, y - 4))
    y_wait(0, 3, 1)
    y_wait(1, 3, 1)
    x_wait(1, y, FIRST, ROWS - FIRST)
    for k, yy in crossed:
        x_wait(k, yy, FIRST, ROWS - FIRST)
    local.wait()
    near_copy.wait()
    low_copy.wait()
    for copy in sent:
        copy.wait_send()


def finish_kernel(
    tile_at,
    kind_at,
    used,
    table,
    group,
    lower_in,
    near_in,
    mask_in,
    p2c,
    recv_map,
    out,
    gb,
    gf,
    ta,
    tb,
    sa,
    sb,
    low_v,
    near_v,
    mask_v,
    sem,
):
    chunks = group.shape[0]
    loads = [pltpu.make_async_copy(group.at[c], gb.at[c], sem.at[c]) for c in range(chunks)]
    rest = [
        pltpu.make_async_copy(src, dst, sem.at[chunks + n])
        for n, (src, dst) in enumerate(((lower_in, low_v), (near_in, near_v), (mask_in, mask_v)))
    ]
    for copy in loads + rest:
        copy.start()

    kinds = table.shape[0] // 4
    zero = jnp.zeros((kinds, 128), F32)
    real = [table[pl.ds(n, kinds, stride=4), :] for n in range(2)]
    imag = [table[pl.ds(2 + n, kinds, stride=4), :] for n in range(2)]
    for par in range(2):
        for row in range(8):
            here = row // 4 == par
            part = row % 4
            at = pl.ds(8 * kinds * par + row, kinds, stride=8)
            ta[at, :] = real[part % 2] if here else zero
            tb[at, :] = (imag[part % 2] if part < 2 else -imag[part % 2]) if here else zero
    ta[pl.ds(16 * kinds, 8), :] = jnp.zeros((8, 128), F32)
    tb[pl.ds(16 * kinds, 8), :] = jnp.zeros((8, 128), F32)

    for c in range(chunks):
        loads[c].wait()
        gf[pl.ds(ROWS * c, ROWS), :] = gb[c].astype(F32)

    def target(t, _):
        def four(q, carry):
            s1, s2 = carry
            for e in range(4):
                at = t * 16 + q * 4 + e
                x = gf[pl.ds(pl.multiple_of(tile_at[at], 8), 8), :]
                kk = pl.multiple_of(kind_at[at], 8)
                s1 = s1 + ta[pl.ds(kk, 8), :] * x
                s2 = s2 + tb[pl.ds(kk, 8), :] * x
            return s1, s2

        zero_tile = jnp.zeros((8, 128), F32)
        s1, s2 = lax.fori_loop(0, used[t], four, (zero_tile, zero_tile))
        rows = pl.ds(pl.multiple_of(8 * t, 8), 8)
        sa[rows, :] = s1
        sb[rows, :] = s2
        return 0

    lax.fori_loop(0, 256, target, 0)

    def take(ref, row):
        return ref[pl.ds(row, 256, stride=8), :] + ref[pl.ds(row + 4, 256, stride=8), :]

    parts = [take(sa, n) + take(sb, (n + 2) % 4) for n in range(4)]
    coarse_in = jnp.concatenate(parts, axis=1).astype(BF16)
    for copy in rest:
        copy.wait()
    for q in range(4):
        got = jnp.dot(coarse_in, p2c[pl.ds(512 * q, 512), :], preferred_element_type=F32)
        for p in range(16):
            rows = pl.ds(64 * p + 16 * q, 16)
            low_v[rows, :] = low_v[rows, :] + got[16 * p : 16 * p + 16]
    for block in range(4):
        rows = pl.ds(256 * block, 256)
        field = jnp.dot(low_v[rows, :].astype(BF16), recv_map[...], preferred_element_type=F32) + near_v[rows, :]
        mask = mask_v[rows, :]
        for h in range(2):
            kept = field[:, 128 * h : 128 * h + 128] * mask
            for n in range(16):
                i = 8 * block + n // 2
                out[pl.ds(64 * i + 2 * (n % 2) + h, 16, stride=4), :] = kept[16 * n : 16 * n + 16]


def body(
    n_gx,
    n_gy,
    currents,
    box_count,
    aggregate,
    near_blocks,
    low_translator,
    child_to_parent,
    coarse_list,
    coarse_kind,
    coarse_count,
    up_translator,
    parent_to_child,
    receive_map,
):
    vmem = pl.BlockSpec(memory_space=pltpu.VMEM)
    smem = pl.BlockSpec(memory_space=pltpu.SMEM)
    anywhere = pl.BlockSpec(memory_space=pl.ANY)
    group, lower, near, mask = pl.pallas_call(
        functools.partial(gather_kernel, n_gx, n_gy),
        name="gather",
        out_shape=(
            jax.ShapeDtypeStruct((n_gy, ROWS, 128), BF16),
            jax.ShapeDtypeStruct((1024, 256), F32),
            jax.ShapeDtypeStruct((1024, 256), F32),
            jax.ShapeDtypeStruct((1024, 128), F32),
        ),
        in_specs=[vmem] * 6,
        out_specs=(anywhere,) * 4,
        scratch_shapes=[
            pltpu.VMEM((2048, 32), BF16),
            pltpu.VMEM((2048, 128), F32),
            pltpu.VMEM((WIDE * PITCH, 128), F32),
            pltpu.VMEM((WIDE * PITCH, 128), F32),
            pltpu.VMEM((WIDE * 64, 256), BF16),
            pltpu.VMEM((1024, 256), BF16),
            pltpu.VMEM((ROWS, 128), F32),
            pltpu.VMEM((ROWS, 128), BF16),
            pltpu.VMEM((WIDE * 8, 128), BF16),
            pltpu.VMEM((WIDE * 8, 128), BF16),
            pltpu.VMEM((WIDE * 8, 128), BF16),
            pltpu.VMEM((WIDE * 8, 128), BF16),
            pltpu.VMEM((1024, 256), F32),
            pltpu.VMEM((1024, 256), F32),
            pltpu.SemaphoreType.DMA((2, 4, 2)),
            pltpu.SemaphoreType.DMA((2, 4, 2)),
            pltpu.SemaphoreType.DMA((9,)),
            pltpu.SemaphoreType.DMA((9,)),
            pltpu.SemaphoreType.DMA((6,)),
            pltpu.SemaphoreType.DMA((6,)),
            pltpu.SemaphoreType.DMA((4,)),
        ],
        compiler_params=pltpu.CompilerParams(
            collective_id=0, has_side_effects=True, vmem_limit_bytes=40 * 1024 * 1024
        ),
    )(
        currents.reshape(2048, 128),
        box_count,
        aggregate,
        near_blocks.reshape(9 * 256, 256),
        low_translator.reshape(32, 128),
        child_to_parent.reshape(1024, 512),
    )

    source = coarse_list.reshape(256, 16)
    tile = (((source >> 4) & 15) << 8) + ((source >> 8) << 4) + (source & 15)
    valid = lax.broadcasted_iota(jnp.int32, (256, 16), 1) < coarse_count.reshape(256, 1)
    kind = coarse_kind.reshape(256, 16) + 64 * (source & 1)
    tile_at = ((tile >> 1) * 8).reshape(4096)
    kind_at = (jnp.where(valid, kind, 128) * 8).reshape(4096)
    used = ((coarse_count + 3) // 4).reshape(256)
    out = pl.pallas_call(
        finish_kernel,
        name="finish",
        out_shape=jax.ShapeDtypeStruct((2048, 128), F32),
        in_specs=[smem, smem, smem, vmem] + [anywhere] * 4 + [vmem, vmem],
        out_specs=vmem,
        scratch_shapes=[
            pltpu.VMEM((n_gy, ROWS, 128), BF16),
            pltpu.VMEM((n_gy * ROWS, 128), F32),
            pltpu.VMEM((129 * 8, 128), F32),
            pltpu.VMEM((129 * 8, 128), F32),
            pltpu.VMEM((2048, 128), F32),
            pltpu.VMEM((2048, 128), F32),
            pltpu.VMEM((1024, 256), F32),
            pltpu.VMEM((1024, 256), F32),
            pltpu.VMEM((1024, 128), F32),
            pltpu.SemaphoreType.DMA((n_gy + 3,)),
        ],
        compiler_params=pltpu.CompilerParams(vmem_limit_bytes=40 * 1024 * 1024),
    )(
        tile_at,
        kind_at,
        used,
        up_translator.reshape(256, 128),
        group,
        lower,
        near,
        mask,
        parent_to_child.reshape(2048, 256),
        receive_map,
    )
    return out.reshape(32, 32, 2, 128)


def solution(mesh):
    in_specs = (
        P("gx", "gy", None, None),
        P("gx", "gy"),
        P(),
        P(),
        P(),
        P(),
        P("gx", "gy", None),
        P("gx", "gy", None),
        P("gx", "gy"),
        P(),
        P(),
        P(),
    )
    out_specs = P("gx", "gy", None, None)
    step = functools.partial(body, mesh.shape["gx"], mesh.shape["gy"])
    return jax.shard_map(step, mesh=mesh, in_specs=in_specs, out_specs=out_specs, check_vma=False)
```

time: 235 us -> 75.7 us (0.32)
  the two profiles are of different devices: /device:TPU:8 before, /device:TPU:16 now
where the time goes in v1:
time: 75.7 us; the launch traced here: 75.3 us
  Pallas kernels  65.2 us (86%)
  local copies, waits for them, and re-layouts  8.14 us (11%)
  other arithmetic  1.85 us (2%)
    pallas_call x1, Pallas kernels, body(): pl.pallas_call(functools.partial(gather_kernel, n_gx, n_gy), name='gather...  49.2 us
    pallas_call x1, Pallas kernels, body(): pl.pallas_call(finish_kernel, name='finish', out_shape=jax.ShapeDtypeStru...  16 us
    unnamed x16, local copies, waits for them, and re-layouts  5.88 us

profile of v1, /device:TPU:16, one launch (start us, length us, event | category | flops | bytes accessed | tf_op | source)
XLA Modules:
  0.0 75.3 jit_solution(10009951361717585154)
XLA Ops:
  0.0 0.0 copy-start.4
  0.0 0.0 copy-start.1
  0.0 0.9 %lt.14 = s32[256]{0:T(256)S(1)} reshape(s32[16,16]{1,0:T(8,128)} %param.20) | data formatting | bytes 2048 | tf_op jit(solution)/shard_map/lt | solution.py:502
  0.9 0.7 add_select_fusion
  1.6 0.1 reshape.54.used
  1.7 0.1 iota_compare_fusion
  1.8 0.1 lt.17
  1.9 1.0 %reshape.55.table = f32[256,128]{1,0:T(8,128)S(1)} reshape(f32[64,2,256]{2,1,0:T(2,128)} %param.21) | data formatting | bytes 262144 | tf_op jit(solution)/shard_map/reshape | solution.py:530
  2.9 1.0 %multiply_add_fusion = (s32[16,16,16]{2,1,0:T(8,128)S(1)}, s32[16,16,16]{2,1,0:T(8,128)S(1)}) fusion(s32[16,16,16]{2,1,0:T(8,128)} %param.19, s32[16,16,16]{2,1,0:T(8,128)} %param.18), kind=kLoop, calls=%fused_computation.1 | loop fusion | flops 53248 | bytes 65536 | tf_op jit(solution)/shard_map/add | solution.py:503
  3.9 0.1 add.29
  4.1 0.1 reshape.66.tile_at
  4.2 0.0 copy-start
  4.2 1.3 %copy-done = bf16[9,256,256]{2,1,0:T(8,128)(2,1)S(1)} copy-done((bf16[9,256,256]{2,1,0:T(8,128)(2,1)S(1)}, bf16[9,256,256]{2,1,0:T(8,128)(2,1)}, u32[]{:S(2)}) %copy-start) | copy-done | bytes 1179672
  5.4 0.0 copy-start.2
  5.4 1.2 %copy-done.2 = bf16[4,256,512]{2,1,0:T(8,128)(2,1)S(1)} copy-done((bf16[4,256,512]{2,1,0:T(8,128)(2,1)S(1)}, bf16[4,256,512]{2,1,0:T(8,128)(2,1)}, u32[]{:S(2)}) %copy-start.2) | copy-done | bytes 1048600
  6.7 0.0 copy-start.3
  6.7 1.0 %copy-done.3 = bf16[32,32,2,128]{3,2,1,0:T(2,128)(2,1)S(1)} copy-done((bf16[32,32,2,128]{3,2,1,0:T(2,128)(2,1)S(1)}, bf16[32,32,2,128]{3,2,1,0:T(2,128)(2,1)}, u32[]{:S(2)}) %copy-start.3) | copy-done | bytes 524312
  7.7 0.0 copy-start.5
  7.7 0.9 %copy-done.5 = bf16[256,256]{1,0:T(8,128)(2,1)S(1)} copy-done((bf16[256,256]{1,0:T(8,128)(2,1)S(1)}, bf16[256,256]{1,0:T(8,128)(2,1)}, u32[]{:S(2)}) %copy-start.5) | copy-done | bytes 131096
  8.6 0.0 copy-start.6
  8.6 0.7 copy-done.6
  9.3 0.0 copy-start.7
  9.3 0.7 copy-done.7
  10.0 49.2 %gather.1 = (bf16[16,1024,128]{2,1,0:T(8,128)(2,1)S(1)}, f32[1024,256]{1,0:T(8,128)S(1)}, f32[1024,256]{1,0:T(8,128)S(1)}, f32[1024,128]{1,0:T(8,128)S(1)}) custom-call(bf16[2048,128]{1,0:T(8,128)(2,1)S(1)} %bitcast.9, s32[32,32]{1,0:T(8,128)S(1)} %copy-done.6, bf16[256,256]{1,0:T(8,128)(2,1)S(1)} %copy-done.5, bf16[2304,256]{1,0:T(8,128)(2,1)S(1)} %bitcast.6, ...), custom_call_target="tpu_custom_call" | custom-call | tf_op jit(solution)/shard_map/gather/pallas_call | solution.py:454
  59.3 0.0 copy-done.4
  59.3 0.0 copy-done.1
  59.3 16.0 %finish.1 = f32[2048,128]{1,0:T(8,128)} custom-call(s32[4096]{0:T(1024)S(1)} %reshape.66.tile_at, s32[4096]{0:T(1024)S(1)} %select_multiply_fusion.kind_at, s32[256]{0:T(256)S(1)} %reshape.54.used, f32[256,128]{1,0:T(8,128)S(1)} %reshape.55.table, bf16[16,1024,128]{2,1,0:T(8,128)(2,1)S(1)} %get-tuple-element.9.group, ...), custom_call_target="tpu_custom_call" | custom-call | tf_op jit(solution)/shard_map/finish/pallas_call | solution.py:507
  (1 shorter events, 0.0 us)
Async XLA Ops:
  0.0 59.3 %copy-start.4 = (bf16[256,256]{1,0:T(8,128)(2,1)S(1)}, bf16[256,256]{1,0:T(8,128)(2,1)}, u32[]{:S(2)}) copy-start(bf16[256,256]{1,0:T(8,128)(2,1)} %recv_map.1) | copy-start | bytes 393220
  0.0 59.3 %copy-start.1 = (bf16[4,512,256]{2,1,0:T(8,128)(2,1)S(1)}, bf16[4,512,256]{2,1,0:T(8,128)(2,1)}, u32[]{:S(2)}) copy-start(bf16[4,512,256]{2,1,0:T(8,128)(2,1)} %param.22) | copy-start | bytes 3145732
  4.2 1.3 %copy-start = (bf16[9,256,256]{2,1,0:T(8,128)(2,1)S(1)}, bf16[9,256,256]{2,1,0:T(8,128)(2,1)}, u32[]{:S(2)}) copy-start(bf16[9,256,256]{2,1,0:T(8,128)(2,1)} %param.15) | copy-start | bytes 3538948
  5.4 1.2 %copy-start.2 = (bf16[4,256,512]{2,1,0:T(8,128)(2,1)S(1)}, bf16[4,256,512]{2,1,0:T(8,128)(2,1)}, u32[]{:S(2)}) copy-start(bf16[4,256,512]{2,1,0:T(8,128)(2,1)} %param.17) | copy-start | bytes 3145732
  6.7 1.0 %copy-start.3 = (bf16[32,32,2,128]{3,2,1,0:T(2,128)(2,1)S(1)}, bf16[32,32,2,128]{3,2,1,0:T(2,128)(2,1)}, u32[]{:S(2)}) copy-start(bf16[32,32,2,128]{3,2,1,0:T(2,128)(2,1)} %param.12) | copy-start | bytes 1572868
  7.7 0.9 %copy-start.5 = (bf16[256,256]{1,0:T(8,128)(2,1)S(1)}, bf16[256,256]{1,0:T(8,128)(2,1)}, u32[]{:S(2)}) copy-start(bf16[256,256]{1,0:T(8,128)(2,1)} %agg.1) | copy-start | bytes 393220
  8.6 0.7 copy-start.6
  9.3 0.7 copy-start.7

commit v2 on v1

--- a/solution.py
+++ b/solution.py
@@ -28,16 +28,36 @@
 def gather_kernel(
     n_gx,
     n_gy,
+    cur_in,
+    cnt_in,
+    agg_in,
+    near_in,
+    low_in,
+    c2p_in,
+    table_in,
+    kind_in,
+    used_in,
+    list_in,
+    order,
+    tiles,
+    factor_r,
+    factor_i,
+    low_v,
+    near_v,
+    mask_v,
     cur,
     cnt,
     agg,
     near,
     low,
     c2p,
+    table,
+    kind,
+    used,
+    source,
     group,
-    lower_out,
-    near_out,
-    mask_out,
+    tables,
+    picks,
     sel_rows,
     cntb,
     lf,
@@ -50,15 +70,13 @@
     s_hi,
     h_lo,
     h_hi,
-    low_v,
-    near_v,
     ys,
     yr,
     xs,
     xr,
     hs,
     hr,
-    loc,
+    ld,
 ):
     gx = lax.axis_index("gx")
     gy = lax.axis_index("gy")
@@ -80,6 +98,24 @@
     barrier = pltpu.get_barrier_semaphore()
     for device in (x_next, x_prev, y_next, y_prev, r_next, r_prev):
         pl.semaphore_signal(barrier, inc=1, device_id=device, device_id_type=MESH)
+
+    pairs = (
+        (cnt_in, cnt),
+        (cur_in, cur),
+        (agg_in, agg),
+        (c2p_in, c2p),
+        (table_in, table),
+        (kind_in, kind),
+        (used_in, used),
+        (near_in, near),
+        (low_in, low),
+        (list_in, source),
+    )
+    loads = [pltpu.make_async_copy(src, dst, ld.at[n]) for n, (src, dst) in enumerate(pairs)]
+    for copy in loads:
+        copy.start()
+    loads[0].wait()
+    loads[1].wait()
 
     pick = (
         lax.broadcasted_iota(jnp.int32, (2 * TY, TY), 0) // 2 == lax.broadcasted_iota(jnp.int32, (2 * TY, TY), 1)
@@ -116,10 +152,12 @@
         for h in range(2):
             pf[pl.ds(PITCH * x + 8 + 2 * b + h, 16, stride=4), :] = value[:, 128 * h : 128 * h + 128]
 
+    loads[2].wait()
     for block in range(4):
         got = jnp.dot(lines(ll, 2 + 8 * block, 8, 1, 2), agg[...], preferred_element_type=F32).astype(BF16)
         pv[pl.ds(256 * block, 256), :] = got
 
+    loads[3].wait()
     total = jnp.zeros((256, 512), F32)
     for q in range(4):
         child = jnp.concatenate([pv[pl.ds(64 * p + 16 * q, 16), :] for p in range(16)], axis=0)
@@ -168,9 +206,6 @@
     y_send(0, 0, 0)
     y_send(1, 0, 0)
     x_send(1, y, FIRST, ROWS - FIRST, True)
-    local = pltpu.make_async_copy(own, group.at[gy], loc.at[0])
-    local.start()
-
     def x_halo(k):
         src = (2, 3, TX, TX + 1)[k]
         dst = (TX + 2, TX + 3, 0, 1)[k]
@@ -186,15 +221,23 @@
     for copy in halo:
         copy.start()
 
+    def unfold(sl, src, first, count):
+        def line(p, _):
+            rows = src[pl.ds(pl.multiple_of(64 * p, 64), 64), :].astype(F32)
+            tiles[pl.ds(pl.multiple_of(1024 * p + 64 * sl, 64), 64), :] = rows
+            return 0
+
+        lax.fori_loop(first // 64, (first + count) // 64, line, 0)
+
+    def unfold_slot(yy, xx, first, count):
+        sl = slot(yy, xx)
+        unfold(sl, group.at[sl], first, count)
+
     own_lane = lax.broadcasted_iota(jnp.int32, (16, 128), 1).astype(F32)
     for i in range(TX):
         for b in range(2):
             held = cntb[pl.ds(64 * i + 2 * b, 16, stride=4), :]
-            mask_out_rows = jnp.where(own_lane < held, 1.0, 0.0)
-            cf_rows = pl.ds(32 * i + 16 * b, 16)
-            low_v[cf_rows, pl.ds(0, 128)] = mask_out_rows
-    mask_copy = pltpu.make_async_copy(low_v.at[:, pl.ds(0, 128)], mask_out, loc.at[1])
-    mask_copy.start()
+            mask_v[pl.ds(32 * i + 16 * b, 16), :] = jnp.where(own_lane < held, 1.0, 0.0)
     for i in range(TX):
         for b in range(2):
             spread(i + 2, b, pv[pl.ds(32 * i + 16 * b, 16), :].astype(F32))
@@ -223,9 +266,48 @@
     for copy in halo_y:
         copy.start()
 
+    for copy in loads[4:]:
+        copy.wait()
+    kinds = table.shape[0] // 4
+    for n in range(4):
+        rest = table[pl.ds(2 * (n % 2) + n // 2, kinds, stride=4), :]
+        for part in range(3):
+            top = rest.astype(BF16)
+            tables[pl.ds(kinds * part, kinds), pl.ds(128 * n, 128)] = top
+            rest = rest - top.astype(F32)
+    square = (lax.broadcasted_iota(jnp.int32, (16, 16), 0) == lax.broadcasted_iota(jnp.int32, (16, 16), 1)).astype(F32)
+    spread_used = [jnp.broadcast_to(used[pl.ds(p, 1), :].astype(F32), (16, 16)) * square for p in range(16)]
+    held_used = jnp.dot(
+        jnp.concatenate(spread_used, axis=0).astype(BF16), jnp.ones((16, 128), BF16), preferred_element_type=F32
+    )
+    entry = lax.broadcasted_iota(jnp.int32, (256, 16), 1).astype(F32)
+    picks[...] = jnp.where(entry < held_used[:, :16], kind[...].astype(F32), -1.0)
+
+    group_of = lax.broadcasted_iota(jnp.int32, (32, 128), 1) // 16
+    dense = jnp.zeros((32, 128), jnp.int32)
+    for u in range(8):
+        some = source[pl.ds(u, 32, stride=8), :]
+        dense = jnp.where(group_of == u, jnp.concatenate([some] * 8, axis=1), dense)
+    order[...] = dense
+
+    def factor_part(e):
+        wide = lax.rem(lax.broadcasted_iota(jnp.int32, (256, 3 * kinds), 1), kinds).astype(F32)
+        choice = jnp.broadcast_to(picks[:, e : e + 1], (256, 3 * kinds)) == wide
+        got = jnp.dot(jnp.where(choice, 1.0, 0.0).astype(BF16), tables[...], preferred_element_type=F32)
+        for row in range(4):
+            at = pl.ds(1024 * e + row, 256, stride=4)
+            n = row % 2
+            factor_r[at, :] = got[:, 128 * n : 128 * n + 128]
+            part = got[:, 256 + 128 * n : 384 + 128 * n]
+            factor_i[at, :] = -part if row >= 2 else part
+
     x_wait(0, y, 0, FIRST)
     y_send(0, 0, 1)
     y_send(1, 0, 1)
+    unfold(gy, own, 0, ROWS)
+    unfold_slot(y, px, 0, FIRST)
+    factor_part(0)
+    factor_part(1)
 
     for x in (0, 1, TX + 2, TX + 3):
         for k in (1, 2):
@@ -266,11 +348,19 @@
     def step(d, w, dr):
         y_wait(dr, d - 1, w)
         y_send(dr, d, w)
+        yy = y - sign[dr] * d
         if w == 0:
             k = 2 + (d - 1) * 2 + dr
-            yy = y - sign[dr] * d
             x_send(k, yy, FIRST, ROWS - FIRST)
             crossed.append((k, yy))
+            unfold_slot(yy, xh, 0, ROWS)
+        else:
+            unfold_slot(yy, px, 0, FIRST)
+
+    def cross_step(n):
+        k, yy = crossed[n]
+        x_wait(k, yy, FIRST, ROWS - FIRST)
+        unfold_slot(yy, px, FIRST, ROWS - FIRST)
 
     def near_chunk(c):
         acc = jnp.zeros((256, 256), F32)
@@ -297,133 +387,95 @@
             low_v[rows, pl.ds(128, 128)] = second
         return 0
 
+    def factor_parts(n):
+        factor_part(2 * n)
+        factor_part(2 * n + 1)
+
+    crossed.append((1, y))
     step(1, 0, 0)
     step(1, 0, 1)
     for x in range(1, WIDE - 1):
         for k in (0, 3):
             plane(x, k)
+    factor_parts(1)
     step(1, 1, 0)
     step(1, 1, 1)
     near_chunk(0)
     near_chunk(1)
+    factor_parts(2)
+    cross_step(0)
     step(2, 0, 0)
     step(2, 0, 1)
     near_chunk(2)
     near_chunk(3)
-    near_copy = pltpu.make_async_copy(near_v, near_out, loc.at[2])
-    near_copy.start()
-    mask_copy.wait()
+    factor_parts(3)
+    cross_step(1)
+    cross_step(2)
     step(2, 1, 0)
     step(2, 1, 1)
     lax.fori_loop(0, TX // 2, lower_line, 0)
+    factor_parts(4)
     step(3, 0, 0)
     step(3, 0, 1)
+    cross_step(3)
+    cross_step(4)
     lax.fori_loop(TX // 2, TX, lower_line, 0)
-    low_copy = pltpu.make_async_copy(low_v, lower_out, loc.at[3])
-    low_copy.start()
+    factor_parts(5)
     step(3, 1, 0)
     step(3, 1, 1)
+    factor_parts(6)
     y_wait(0, 3, 0)
     y_wait(1, 3, 0)
     x_send(8, y - 4, FIRST, ROWS - FIRST)
     crossed.append((8, y - 4))
+    unfold_slot(y - 4, xh, 0, ROWS)
+    factor_parts(7)
+    cross_step(5)
+    cross_step(6)
     y_wait(0, 3, 1)
     y_wait(1, 3, 1)
-    x_wait(1, y, FIRST, ROWS - FIRST)
-    for k, yy in crossed:
-        x_wait(k, yy, FIRST, ROWS - FIRST)
-    local.wait()
-    near_copy.wait()
-    low_copy.wait()
+    unfold_slot(y - 4, px, 0, FIRST)
+    cross_step(7)
     for copy in sent:
         copy.wait_send()
 
 
-def finish_kernel(
-    tile_at,
-    kind_at,
-    used,
-    table,
-    group,
-    lower_in,
-    near_in,
-    mask_in,
-    p2c,
-    recv_map,
-    out,
-    gb,
-    gf,
-    ta,
-    tb,
-    sa,
-    sb,
-    low_v,
-    near_v,
-    mask_v,
-    sem,
-):
-    chunks = group.shape[0]
-    loads = [pltpu.make_async_copy(group.at[c], gb.at[c], sem.at[c]) for c in range(chunks)]
-    rest = [
-        pltpu.make_async_copy(src, dst, sem.at[chunks + n])
-        for n, (src, dst) in enumerate(((lower_in, low_v), (near_in, near_v), (mask_in, mask_v)))
-    ]
-    for copy in loads + rest:
+def finish_kernel(order, tiles, factor_r, factor_i, low_v, near_v, mask_v, p2c_in, recv_in, out, sums, incoming, p2c, recv_map, sem):
+    loads = [pltpu.make_async_copy(p2c_in, p2c, sem.at[0]), pltpu.make_async_copy(recv_in, recv_map, sem.at[1])]
+    for copy in loads:
         copy.start()
 
-    kinds = table.shape[0] // 4
-    zero = jnp.zeros((kinds, 128), F32)
-    real = [table[pl.ds(n, kinds, stride=4), :] for n in range(2)]
-    imag = [table[pl.ds(2 + n, kinds, stride=4), :] for n in range(2)]
-    for par in range(2):
-        for row in range(8):
-            here = row // 4 == par
-            part = row % 4
-            at = pl.ds(8 * kinds * par + row, kinds, stride=8)
-            ta[at, :] = real[part % 2] if here else zero
-            tb[at, :] = (imag[part % 2] if part < 2 else -imag[part % 2]) if here else zero
-    ta[pl.ds(16 * kinds, 8), :] = jnp.zeros((8, 128), F32)
-    tb[pl.ds(16 * kinds, 8), :] = jnp.zeros((8, 128), F32)
-
-    for c in range(chunks):
-        loads[c].wait()
-        gf[pl.ds(ROWS * c, ROWS), :] = gb[c].astype(F32)
-
-    def target(t, _):
-        def four(q, carry):
-            s1, s2 = carry
-            for e in range(4):
-                at = t * 16 + q * 4 + e
-                x = gf[pl.ds(pl.multiple_of(tile_at[at], 8), 8), :]
-                kk = pl.multiple_of(kind_at[at], 8)
-                s1 = s1 + ta[pl.ds(kk, 8), :] * x
-                s2 = s2 + tb[pl.ds(kk, 8), :] * x
-            return s1, s2
-
-        zero_tile = jnp.zeros((8, 128), F32)
-        s1, s2 = lax.fori_loop(0, used[t], four, (zero_tile, zero_tile))
-        rows = pl.ds(pl.multiple_of(8 * t, 8), 8)
-        sa[rows, :] = s1
-        sb[rows, :] = s2
+    def targets(n, _):
+        for u in range(8):
+            t = 8 * n + u
+            first = jnp.zeros((4, 128), F32)
+            second = jnp.zeros((4, 128), F32)
+            for e in range(16):
+                x = tiles[order[n, 16 * u + e]]
+                first = first + factor_r[t + 256 * e] * x
+                second = second + factor_i[t + 256 * e] * x
+            rows = pl.multiple_of(8 * t, 8)
+            sums[pl.ds(rows, 4), :] = first
+            sums[pl.ds(rows + 4, 4), :] = second
         return 0
 
-    lax.fori_loop(0, 256, target, 0)
-
-    def take(ref, row):
-        return ref[pl.ds(row, 256, stride=8), :] + ref[pl.ds(row + 4, 256, stride=8), :]
-
-    parts = [take(sa, n) + take(sb, (n + 2) % 4) for n in range(4)]
+    lax.fori_loop(0, 32, targets, 0)
+
+    def take(row):
+        return sums[pl.ds(row, 256, stride=8), :]
+
+    parts = [take(0) + take(6), take(1) + take(7), take(2) + take(4), take(3) + take(5)]
     coarse_in = jnp.concatenate(parts, axis=1).astype(BF16)
-    for copy in rest:
+    for copy in loads:
         copy.wait()
     for q in range(4):
         got = jnp.dot(coarse_in, p2c[pl.ds(512 * q, 512), :], preferred_element_type=F32)
         for p in range(16):
             rows = pl.ds(64 * p + 16 * q, 16)
-            low_v[rows, :] = low_v[rows, :] + got[16 * p : 16 * p + 16]
+            incoming[rows, :] = (low_v[rows, :] + got[16 * p : 16 * p + 16]).astype(BF16)
     for block in range(4):
         rows = pl.ds(256 * block, 256)
-        field = jnp.dot(low_v[rows, :].astype(BF16), recv_map[...], preferred_element_type=F32) + near_v[rows, :]
+        field = jnp.dot(incoming[rows, :], recv_map[...], preferred_element_type=F32) + near_v[rows, :]
         mask = mask_v[rows, :]
         for h in range(2):
             kept = field[:, 128 * h : 128 * h + 128] * mask
@@ -448,92 +500,101 @@
     parent_to_child,
     receive_map,
 ):
-    vmem = pl.BlockSpec(memory_space=pltpu.VMEM)
-    smem = pl.BlockSpec(memory_space=pltpu.SMEM)
-    anywhere = pl.BlockSpec(memory_space=pl.ANY)
-    group, lower, near, mask = pl.pallas_call(
+    vmem = pltpu.VMEM
+    held = pl.BlockSpec(memory_space=pltpu.HBM)
+    near_by = pl.BlockSpec(memory_space=pltpu.VMEM)
+    order, tiles, factor_r, factor_i, lower, near, mask = pl.pallas_call(
         functools.partial(gather_kernel, n_gx, n_gy),
         name="gather",
         out_shape=(
-            jax.ShapeDtypeStruct((n_gy, ROWS, 128), BF16),
+            jax.ShapeDtypeStruct((32, 128), jnp.int32),
+            jax.ShapeDtypeStruct((16384, 128), F32),
+            jax.ShapeDtypeStruct((16384, 128), F32),
+            jax.ShapeDtypeStruct((16384, 128), F32),
             jax.ShapeDtypeStruct((1024, 256), F32),
             jax.ShapeDtypeStruct((1024, 256), F32),
             jax.ShapeDtypeStruct((1024, 128), F32),
         ),
-        in_specs=[vmem] * 6,
-        out_specs=(anywhere,) * 4,
+        in_specs=[held] * 10,
+        out_specs=(near_by,) * 7,
         scratch_shapes=[
-            pltpu.VMEM((2048, 32), BF16),
-            pltpu.VMEM((2048, 128), F32),
-            pltpu.VMEM((WIDE * PITCH, 128), F32),
-            pltpu.VMEM((WIDE * PITCH, 128), F32),
-            pltpu.VMEM((WIDE * 64, 256), BF16),
-            pltpu.VMEM((1024, 256), BF16),
-            pltpu.VMEM((ROWS, 128), F32),
-            pltpu.VMEM((ROWS, 128), BF16),
-            pltpu.VMEM((WIDE * 8, 128), BF16),
-            pltpu.VMEM((WIDE * 8, 128), BF16),
-            pltpu.VMEM((WIDE * 8, 128), BF16),
-            pltpu.VMEM((WIDE * 8, 128), BF16),
-            pltpu.VMEM((1024, 256), F32),
-            pltpu.VMEM((1024, 256), F32),
+            vmem((2048, 128), BF16),
+            vmem((32, 32), jnp.int32),
+            vmem((256, 256), BF16),
+            vmem((2304, 256), BF16),
+            vmem((32, 128), F32),
+            vmem((1024, 512), BF16),
+            vmem((256, 128), F32),
+            vmem((256, 16), jnp.int32),
+            vmem((16, 16), jnp.int32),
+            vmem((256, 16), jnp.int32),
+            vmem((n_gy, ROWS, 128), BF16),
+            vmem((192, 512), BF16),
+            vmem((256, 16), F32),
+            vmem((2048, 32), BF16),
+            vmem((2048, 128), F32),
+            vmem((WIDE * PITCH, 128), F32),
+            vmem((WIDE * PITCH, 128), F32),
+            vmem((WIDE * 64, 256), BF16),
+            vmem((1024, 256), BF16),
+            vmem((ROWS, 128), F32),
+            vmem((ROWS, 128), BF16),
+            vmem((WIDE * 8, 128), BF16),
+            vmem((WIDE * 8, 128), BF16),
+            vmem((WIDE * 8, 128), BF16),
+            vmem((WIDE * 8, 128), BF16),
             pltpu.SemaphoreType.DMA((2, 4, 2)),
             pltpu.SemaphoreType.DMA((2, 4, 2)),
             pltpu.SemaphoreType.DMA((9,)),
             pltpu.SemaphoreType.DMA((9,)),
             pltpu.SemaphoreType.DMA((6,)),
             pltpu.SemaphoreType.DMA((6,)),
-            pltpu.SemaphoreType.DMA((4,)),
+            pltpu.SemaphoreType.DMA((10,)),
         ],
         compiler_params=pltpu.CompilerParams(
-            collective_id=0, has_side_effects=True, vmem_limit_bytes=40 * 1024 * 1024
+            collective_id=0, has_side_effects=True, vmem_limit_bytes=16 * 1024 * 1024
         ),
     )(
-        currents.reshape(2048, 128),
-        box_count,
-        aggregate,
-        near_blocks.reshape(9 * 256, 256),
-        low_translator.reshape(32, 128),
-        child_to_parent.reshape(1024, 512),
+        *(
+            pltpu.with_memory_space_constraint(array, pltpu.HBM)
+            for array in (
+                currents.reshape(2048, 128),
+                box_count,
+                aggregate,
+                near_blocks.reshape(2304, 256),
+                low_translator.reshape(32, 128),
+                child_to_parent.reshape(1024, 512),
+                up_translator.reshape(64, 2, 2, 128).transpose(0, 2, 1, 3).reshape(256, 128),
+                coarse_kind.reshape(256, 16),
+                coarse_count,
+                coarse_list.reshape(256, 16),
+            )
+        )
     )
-
-    source = coarse_list.reshape(256, 16)
-    tile = (((source >> 4) & 15) << 8) + ((source >> 8) << 4) + (source & 15)
-    valid = lax.broadcasted_iota(jnp.int32, (256, 16), 1) < coarse_count.reshape(256, 1)
-    kind = coarse_kind.reshape(256, 16) + 64 * (source & 1)
-    tile_at = ((tile >> 1) * 8).reshape(4096)
-    kind_at = (jnp.where(valid, kind, 128) * 8).reshape(4096)
-    used = ((coarse_count + 3) // 4).reshape(256)
     out = pl.pallas_call(
         finish_kernel,
         name="finish",
         out_shape=jax.ShapeDtypeStruct((2048, 128), F32),
-        in_specs=[smem, smem, smem, vmem] + [anywhere] * 4 + [vmem, vmem],
-        out_specs=vmem,
+        in_specs=[pl.BlockSpec(memory_space=pltpu.SMEM)] + [near_by] * 6 + [held] * 2,
+        out_specs=near_by,
         scratch_shapes=[
-            pltpu.VMEM((n_gy, ROWS, 128), BF16),
-            pltpu.VMEM((n_gy * ROWS, 128), F32),
-            pltpu.VMEM((129 * 8, 128), F32),
-            pltpu.VMEM((129 * 8, 128), F32),
-            pltpu.VMEM((2048, 128), F32),
-            pltpu.VMEM((2048, 128), F32),
-            pltpu.VMEM((1024, 256), F32),
-            pltpu.VMEM((1024, 256), F32),
-            pltpu.VMEM((1024, 128), F32),
-            pltpu.SemaphoreType.DMA((n_gy + 3,)),
+            vmem((2048, 128), F32),
+            vmem((1024, 256), BF16),
+            vmem((2048, 256), BF16),
+            vmem((256, 256), BF16),
+            pltpu.SemaphoreType.DMA((2,)),
         ],
-        compiler_params=pltpu.CompilerParams(vmem_limit_bytes=40 * 1024 * 1024),
+        compiler_params=pltpu.CompilerParams(vmem_limit_bytes=6 * 1024 * 1024),
     )(
-        tile_at,
-        kind_at,
-        used,
-        up_translator.reshape(256, 128),
-        group,
+        order,
+        tiles.reshape(4096, 4, 128),
+        factor_r.reshape(4096, 4, 128),
+        factor_i.reshape(4096, 4, 128),
         lower,
         near,
         mask,
-        parent_to_child.reshape(2048, 256),
-        receive_map,
+        pltpu.with_memory_space_constraint(parent_to_child.reshape(2048, 256), pltpu.HBM),
+        pltpu.with_memory_space_constraint(receive_map, pltpu.HBM),
     )
     return out.reshape(32, 32, 2, 128)
 

time: 75.7 us -> 57 us (0.75)
  Pallas kernels: 65.2 us -> 56.8 us
  local copies, waits for them, and re-layouts: 8.14 us -> 0 us
  other arithmetic: 1.85 us -> 0 us
    pallas_call x1, Pallas kernels: 16 us -> 7.39 us  [body(): pl.pallas_call(finish_kernel, name='finish', out_shape=jax.ShapeDtypeStru...]
    unnamed x16 -> x0, local copies, waits for them, and re-layouts: 5.88 us -> none
    reshape x2 -> x0, local copies, waits for them, and re-layouts: 1.1 us -> none  [the longest x1 1.01 us: body(): up_translator.reshape(256, 128)]
    add x1 -> x0, other arithmetic: 1.03 us -> none  [body(): kind = coarse_kind.reshape(256, 16) + 64 * (source & 1)]
    lt x2 -> x0, local copies, waits for them, and re-layouts: 0.98 us -> none  [body(): lax.broadcasted_iota(jnp.int32, (256, 16), 1) < coarse_count.reshape(256, 1)]
where the time goes in v2:
time: 57 us; the launch traced here: 56.9 us
  Pallas kernels  56.8 us (100%)
    pallas_call x1, Pallas kernels, body(): pl.pallas_call(functools.partial(gather_kernel, n_gx, n_gy), name='gather...  49.5 us
    pallas_call x1, Pallas kernels, body(): pl.pallas_call(finish_kernel, name='finish', out_shape=jax.ShapeDtypeStru...  7.39 us

profile of v2, /device:TPU:16, one launch (start us, length us, event | category | flops | bytes accessed | tf_op | source)
XLA Modules:
  0.0 56.9 jit_solution(2789061937822003108)
XLA Ops:
  0.0 49.5 %gather.1 = (s32[32,128]{1,0:T(8,128)S(1)}, f32[16384,128]{1,0:T(8,128)S(1)}, f32[16384,128]{1,0:T(8,128)S(1)}, f32[16384,128]{1,0:T(8,128)S(1)}, f32[1024,256]{...) custom-call(bf16[2048,128]{1,0:T(8,128)(2,1)} %bitcast.22, s32[32,32]{1,0:T(8,128)} %cnt_in.1, ...), custom_call_target="tpu_custom_call" | custom-call | tf_op jit(solution)/shard_map/gather/pallas_call | solution.py:506
  49.5 7.4 %finish.1 = f32[2048,128]{1,0:T(8,128)} custom-call(s32[32,128]{1,0:T(8,128)S(1)} %get-tuple-element.12.order, f32[4096,4,128]{2,1,0:T(4,128)S(1)} %bitcast.16, f32[4096,4,128]{2,1,0:T(4,128)S(1)} %bitcast.17, f32[4096,4,128]{2,1,0:T(4,128)S(1)} %bitcast.18, f32[1024,256]{1,0:T(8,128)S(1)} %get-tuple-element.16.low_v, ...), custom_call_target="tpu_custom_call" | custom-call | tf_op jit(solution)/shard_map/finish/pallas_call | solution.py:574

commit v3 on v2

--- a/solution.py
+++ b/solution.py
@@ -16,6 +16,10 @@
 WIDE = TX + 4
 ROWS = 1024
 FIRST = 448
+HALF = FIRST // 2
+REST = (ROWS - FIRST) // 2
+OWN = ((FIRST, REST), (FIRST + REST, REST), (0, HALF), (HALF, HALF))
+OTHER = ((0, HALF), (HALF, HALF))
 OFFSETS = [(dx, dy) for dx in range(-2, 3) for dy in range(-2, 3) if max(abs(dx), abs(dy)) == 2]
 
 
@@ -112,10 +116,12 @@
         (list_in, source),
     )
     loads = [pltpu.make_async_copy(src, dst, ld.at[n]) for n, (src, dst) in enumerate(pairs)]
-    for copy in loads:
+    for copy in loads[:4]:
         copy.start()
     loads[0].wait()
     loads[1].wait()
+    for copy in loads[4:]:
+        copy.start()
 
     pick = (
         lax.broadcasted_iota(jnp.int32, (2 * TY, TY), 0) // 2 == lax.broadcasted_iota(jnp.int32, (2 * TY, TY), 1)
@@ -176,36 +182,42 @@
         copy.start()
         sent.append(copy)
 
-    def span(dr, d, w):
-        n = ROWS if w == 0 else FIRST
-        if d < 3:
-            return 0, n
-        return (0, n // 2) if dr == 0 else (n // 2, n - n // 2)
-
-    def y_send(dr, d, w):
-        start, n = span(dr, d, w)
-        where = group.at[slot(y - sign[dr] * d, xh if w == 0 else px), pl.ds(start, n)]
-        src = own.at[pl.ds(start, n)] if (d == 0 and w == 0) else where
-        go(remote(src, where, ys.at[dr, d, w], yr.at[dr, d, w], along[dr]))
-
-    def y_wait(dr, d, w):
-        start, n = span(dr, d, w)
-        where = group.at[slot(y - sign[dr] * (d + 1), xh if w == 0 else px), pl.ds(start, n)]
-        remote(where, where, ys.at[dr, d, w], yr.at[dr, d, w], along[dr]).wait_recv()
-
-    def x_send(k, yy, start, n, mine=False):
-        where = group.at[slot(yy, xh), pl.ds(start, n)]
+    def y_copy(dr, d, w, i, mine=False):
+        start, n = (OTHER if w else OWN)[i]
+        where = group.at[slot(y - sign[dr] * d, px if w else xh), pl.ds(start, n)]
+        k = i + len(OWN) * w
         src = own.at[pl.ds(start, n)] if mine else where
-        go(remote(src, where, xs.at[k], xr.at[k], r_cross))
-
-    def x_wait(k, yy, start, n):
-        where = group.at[slot(yy, px), pl.ds(start, n)]
-        remote(where, where, xs.at[k], xr.at[k], r_cross).wait_recv()
-
-    x_send(0, y, 0, FIRST, True)
-    y_send(0, 0, 0)
-    y_send(1, 0, 0)
-    x_send(1, y, FIRST, ROWS - FIRST, True)
+        return remote(src, where, ys.at[dr, d, k], yr.at[dr, d, k], along[dr])
+
+    def y_arrival(dr, d, w, i):
+        start, n = (OTHER if w else OWN)[i]
+        where = group.at[slot(y - sign[dr] * (d + 1), px if w else xh), pl.ds(start, n)]
+        k = i + len(OWN) * w
+        return remote(where, where, ys.at[dr, d, k], yr.at[dr, d, k], along[dr])
+
+    def turns(d, i):
+        return (0, 1) if d < 3 else (i % 2,)
+
+    def x_copy(j, yy, k, piece, mine=False):
+        where = group.at[slot(yy, xh), pl.ds(*piece)]
+        src = own.at[pl.ds(*piece)] if mine else where
+        return remote(src, where, xs.at[j, k], xr.at[j, k], r_cross)
+
+    def x_arrival(j, yy, k, piece):
+        where = group.at[slot(yy, px), pl.ds(*piece)]
+        return remote(where, where, xs.at[j, k], xr.at[j, k], r_cross)
+
+    def number(d, dr):
+        return 0 if d == 0 else 7 if d == 4 else 1 + 2 * (d - 1) + dr
+
+    for i in range(len(OTHER)):
+        go(x_copy(0, y, 2 + i, OTHER[i], True))
+    for i in range(len(OWN)):
+        for dr in range(2):
+            go(y_copy(dr, 0, 0, i, True))
+    for i in range(2):
+        go(x_copy(0, y, i, OWN[i], True))
+
     def x_halo(k):
         src = (2, 3, TX, TX + 1)[k]
         dst = (TX + 2, TX + 3, 0, 1)[k]
@@ -301,13 +313,43 @@
             part = got[:, 256 + 128 * n : 384 + 128 * n]
             factor_i[at, :] = -part if row >= 2 else part
 
-    x_wait(0, y, 0, FIRST)
-    y_send(0, 0, 1)
-    y_send(1, 0, 1)
+    def own_step(d):
+        for i in range(len(OWN)):
+            for dr in turns(d - 1, i):
+                y_arrival(dr, d - 1, 0, i).wait_recv()
+                if i < 2:
+                    go(x_copy(number(d, dr), y - sign[dr] * d, i, OWN[i]))
+            if d < 4:
+                for dr in turns(d, i):
+                    go(y_copy(dr, d, 0, i))
+        for dr in range(2 if d < 4 else 1):
+            unfold_slot(y - sign[dr] * d, xh, 0, ROWS)
+
+    def other_step(d):
+        for i in range(len(OTHER)):
+            if d == 0:
+                x_arrival(0, y, 2 + i, OTHER[i]).wait_recv()
+            else:
+                for dr in turns(d - 1, i):
+                    y_arrival(dr, d - 1, 1, i).wait_recv()
+            if d < 4:
+                for dr in turns(d, i):
+                    go(y_copy(dr, d, 1, i))
+        for dr in range(2 if 0 < d < 4 else 1):
+            unfold_slot(y - sign[dr] * d, px, 0, FIRST)
+
+    def cross_step(d):
+        for i in range(2):
+            for dr in (0,) if d == 0 else turns(d - 1, i):
+                x_arrival(number(d, dr), y - sign[dr] * d, i, OWN[i]).wait_recv()
+        for dr in range(2 if 0 < d < 4 else 1):
+            unfold_slot(y - sign[dr] * d, px, FIRST, ROWS - FIRST)
+
     unfold(gy, own, 0, ROWS)
-    unfold_slot(y, px, 0, FIRST)
-    factor_part(0)
-    factor_part(1)
+    for e in range(4):
+        factor_part(e)
+    own_step(1)
+    other_step(0)
 
     for x in (0, 1, TX + 2, TX + 3):
         for k in (1, 2):
@@ -342,25 +384,6 @@
         got = jnp.dot(lhs, agg[...], preferred_element_type=F32).astype(BF16).astype(F32)
         for h in range(2):
             pf[pl.ds(start + h, WIDE, stride=PITCH), :] = got[:WIDE, 128 * h : 128 * h + 128]
-
-    crossed = []
-
-    def step(d, w, dr):
-        y_wait(dr, d - 1, w)
-        y_send(dr, d, w)
-        yy = y - sign[dr] * d
-        if w == 0:
-            k = 2 + (d - 1) * 2 + dr
-            x_send(k, yy, FIRST, ROWS - FIRST)
-            crossed.append((k, yy))
-            unfold_slot(yy, xh, 0, ROWS)
-        else:
-            unfold_slot(yy, px, 0, FIRST)
-
-    def cross_step(n):
-        k, yy = crossed[n]
-        x_wait(k, yy, FIRST, ROWS - FIRST)
-        unfold_slot(yy, px, FIRST, ROWS - FIRST)
 
     def near_chunk(c):
         acc = jnp.zeros((256, 256), F32)
@@ -387,60 +410,40 @@
             low_v[rows, pl.ds(128, 128)] = second
         return 0
 
-    def factor_parts(n):
-        factor_part(2 * n)
-        factor_part(2 * n + 1)
-
-    crossed.append((1, y))
-    step(1, 0, 0)
-    step(1, 0, 1)
     for x in range(1, WIDE - 1):
         for k in (0, 3):
             plane(x, k)
-    factor_parts(1)
-    step(1, 1, 0)
-    step(1, 1, 1)
     near_chunk(0)
     near_chunk(1)
-    factor_parts(2)
+    factor_part(4)
+    factor_part(5)
+    own_step(2)
+    other_step(1)
     cross_step(0)
-    step(2, 0, 0)
-    step(2, 0, 1)
     near_chunk(2)
     near_chunk(3)
-    factor_parts(3)
+    for e in range(6, 9):
+        factor_part(e)
     cross_step(1)
+    own_step(3)
+    other_step(2)
+    lax.fori_loop(0, TX // 2, lower_line, 0)
+    for e in range(9, 12):
+        factor_part(e)
     cross_step(2)
-    step(2, 1, 0)
-    step(2, 1, 1)
-    lax.fori_loop(0, TX // 2, lower_line, 0)
-    factor_parts(4)
-    step(3, 0, 0)
-    step(3, 0, 1)
+    own_step(4)
+    other_step(3)
+    lax.fori_loop(TX // 2, TX, lower_line, 0)
+    for e in range(12, 16):
+        factor_part(e)
     cross_step(3)
+    other_step(4)
     cross_step(4)
-    lax.fori_loop(TX // 2, TX, lower_line, 0)
-    factor_parts(5)
-    step(3, 1, 0)
-    step(3, 1, 1)
-    factor_parts(6)
-    y_wait(0, 3, 0)
-    y_wait(1, 3, 0)
-    x_send(8, y - 4, FIRST, ROWS - FIRST)
-    crossed.append((8, y - 4))
-    unfold_slot(y - 4, xh, 0, ROWS)
-    factor_parts(7)
-    cross_step(5)
-    cross_step(6)
-    y_wait(0, 3, 1)
-    y_wait(1, 3, 1)
-    unfold_slot(y - 4, px, 0, FIRST)
-    cross_step(7)
     for copy in sent:
         copy.wait_send()
 
 
-def finish_kernel(order, tiles, factor_r, factor_i, low_v, near_v, mask_v, p2c_in, recv_in, out, sums, incoming, p2c, recv_map, sem):
+def finish_kernel(order, tiles, factor_r, factor_i, low_v, near_v, mask_v, p2c_in, recv_in, result, sums, incoming, p2c, recv_map, out, sem):
     loads = [pltpu.make_async_copy(p2c_in, p2c, sem.at[0]), pltpu.make_async_copy(recv_in, recv_map, sem.at[1])]
     for copy in loads:
         copy.start()
@@ -482,6 +485,13 @@
             for n in range(16):
                 i = 8 * block + n // 2
                 out[pl.ds(64 * i + 2 * (n % 2) + h, 16, stride=4), :] = kept[16 * n : 16 * n + 16]
+        done = pltpu.make_async_copy(
+            out.at[pl.ds(512 * block, 512)], result.at[pl.ds(512 * block, 512)], sem.at[2 + block]
+        )
+        done.start()
+        loads.append(done)
+    for copy in loads[2:]:
+        copy.wait()
 
 
 def body(
@@ -543,10 +553,10 @@
             vmem((WIDE * 8, 128), BF16),
             vmem((WIDE * 8, 128), BF16),
             vmem((WIDE * 8, 128), BF16),
-            pltpu.SemaphoreType.DMA((2, 4, 2)),
-            pltpu.SemaphoreType.DMA((2, 4, 2)),
-            pltpu.SemaphoreType.DMA((9,)),
-            pltpu.SemaphoreType.DMA((9,)),
+            pltpu.SemaphoreType.DMA((2, 4, 6)),
+            pltpu.SemaphoreType.DMA((2, 4, 6)),
+            pltpu.SemaphoreType.DMA((8, 4)),
+            pltpu.SemaphoreType.DMA((8, 4)),
             pltpu.SemaphoreType.DMA((6,)),
             pltpu.SemaphoreType.DMA((6,)),
             pltpu.SemaphoreType.DMA((10,)),
@@ -576,13 +586,14 @@
         name="finish",
         out_shape=jax.ShapeDtypeStruct((2048, 128), F32),
         in_specs=[pl.BlockSpec(memory_space=pltpu.SMEM)] + [near_by] * 6 + [held] * 2,
-        out_specs=near_by,
+        out_specs=held,
         scratch_shapes=[
             vmem((2048, 128), F32),
             vmem((1024, 256), BF16),
             vmem((2048, 256), BF16),
             vmem((256, 256), BF16),
-            pltpu.SemaphoreType.DMA((2,)),
+            vmem((2048, 128), F32),
+            pltpu.SemaphoreType.DMA((6,)),
         ],
         compiler_params=pltpu.CompilerParams(vmem_limit_bytes=6 * 1024 * 1024),
     )(

time: 57 us -> 54.6 us (0.958)
  the two profiles are of different devices: /device:TPU:16 before, /device:TPU:8 now
where the time goes in v3:
time: 54.6 us; the launch traced here: 54.4 us
  Pallas kernels  54.4 us (100%)
    pallas_call x1, Pallas kernels, body(): pl.pallas_call(functools.partial(gather_kernel, n_gx, n_gy), name='gather...  47 us
    pallas_call x1, Pallas kernels, body(): pl.pallas_call(finish_kernel, name='finish', out_shape=jax.ShapeDtypeStru...  7.35 us

profile of v3, /device:TPU:8, one launch (start us, length us, event | category | flops | bytes accessed | tf_op | source)
XLA Modules:
  0.0 54.4 jit_solution(8212262656229780459)
XLA Ops:
  0.0 47.0 %gather.1 = (s32[32,128]{1,0:T(8,128)S(1)}, f32[16384,128]{1,0:T(8,128)S(1)}, f32[16384,128]{1,0:T(8,128)S(1)}, f32[16384,128]{1,0:T(8,128)S(1)}, f32[1024,256]{...) custom-call(bf16[2048,128]{1,0:T(8,128)(2,1)} %bitcast.22, s32[32,32]{1,0:T(8,128)} %cnt_in.1, ...), custom_call_target="tpu_custom_call" | custom-call | tf_op jit(solution)/shard_map/gather/pallas_call | solution.py:516
  47.0 7.3 %finish.1 = f32[2048,128]{1,0:T(8,128)} custom-call(s32[32,128]{1,0:T(8,128)S(1)} %get-tuple-element.12.order, f32[4096,4,128]{2,1,0:T(4,128)S(1)} %bitcast.16, f32[4096,4,128]{2,1,0:T(4,128)S(1)} %bitcast.17, f32[4096,4,128]{2,1,0:T(4,128)S(1)} %bitcast.18, f32[1024,256]{1,0:T(8,128)S(1)} %get-tuple-element.16.low_v, ...), custom_call_target="tpu_custom_call" | custom-call | tf_op jit(solution)/shard_map/finish/pallas_call | solution.py:584

commit v4 on v3

--- a/solution.py
+++ b/solution.py
@@ -14,12 +14,10 @@
 TY = 32
 PITCH = 80
 WIDE = TX + 4
-ROWS = 1024
-FIRST = 448
-HALF = FIRST // 2
-REST = (ROWS - FIRST) // 2
-OWN = ((FIRST, REST), (FIRST + REST, REST), (0, HALF), (HALF, HALF))
-OTHER = ((0, HALF), (HALF, HALF))
+CELLS = 256
+LATER = 144
+OWN = ((0, 80), (80, 64), (144, 64), (208, 48))
+OTHER = OWN[2:]
 OFFSETS = [(dx, dy) for dx in range(-2, 3) for dy in range(-2, 3) if max(abs(dx), abs(dy)) == 2]
 
 
@@ -68,7 +66,6 @@
     pf,
     ll,
     pv,
-    cf,
     own,
     s_lo,
     s_hi,
@@ -131,10 +128,6 @@
         sel_rows[pl.ds(2 * TY * i, 2 * TY), :] = (line * pick).astype(BF16)
     cntb[...] = jnp.dot(sel_rows[...], jnp.ones((TY, 128), BF16), preferred_element_type=F32)
     lane = lax.broadcasted_iota(jnp.int32, (2 * TY, 128), 1).astype(F32)
-    for i in range(TX):
-        rows = pl.ds(2 * TY * i, 2 * TY)
-        live = jnp.where(lane < cntb[rows, :], cur[rows, :].astype(F32), 0.0)
-        lf[pl.ds(PITCH * (i + 2) + 8, 2 * TY), :] = live
 
     def piece(ref, x, start):
         real = ref[pl.ds(PITCH * x + start, 16, stride=4), :]
@@ -146,10 +139,6 @@
         base = 64 * x + 16 * k
         ll[pl.ds(base, 16), :] = jnp.concatenate([real, imag], axis=1).astype(BF16)
 
-    for i in range(TX):
-        for k in (1, 2):
-            plane(i + 2, k)
-
     def lines(ref, x, count, k, planes):
         parts = [ref[pl.ds(64 * (x + n) + 16 * k, 16 * planes), :] for n in range(count)]
         return jnp.concatenate(parts, axis=0)
@@ -157,22 +146,6 @@
     def spread(x, b, value):
         for h in range(2):
             pf[pl.ds(PITCH * x + 8 + 2 * b + h, 16, stride=4), :] = value[:, 128 * h : 128 * h + 128]
-
-    loads[2].wait()
-    for block in range(4):
-        got = jnp.dot(lines(ll, 2 + 8 * block, 8, 1, 2), agg[...], preferred_element_type=F32).astype(BF16)
-        pv[pl.ds(256 * block, 256), :] = got
-
-    loads[3].wait()
-    total = jnp.zeros((256, 512), F32)
-    for q in range(4):
-        child = jnp.concatenate([pv[pl.ds(64 * p + 16 * q, 16), :] for p in range(16)], axis=0)
-        total = total + jnp.dot(child, c2p[pl.ds(256 * q, 256), :], preferred_element_type=F32)
-    for q in range(4):
-        cf[pl.ds(q, 256, stride=4), :] = total[:, 128 * q : 128 * q + 128]
-    own[...] = cf[...].astype(BF16)
-
-    pl.semaphore_wait(barrier, 6)
 
     sign = (1, -1)
     along = (r_next, r_prev)
@@ -210,13 +183,35 @@
     def number(d, dr):
         return 0 if d == 0 else 7 if d == 4 else 1 + 2 * (d - 1) + dr
 
-    for i in range(len(OTHER)):
-        go(x_copy(0, y, 2 + i, OTHER[i], True))
-    for i in range(len(OWN)):
-        for dr in range(2):
-            go(y_copy(dr, 0, 0, i, True))
-    for i in range(2):
-        go(x_copy(0, y, i, OWN[i], True))
+    for part, (low_p, high_p) in enumerate(((0, LATER // 16), (LATER // 16, 16))):
+        for i in range(2 * low_p, 2 * high_p):
+            rows = pl.ds(2 * TY * i, 2 * TY)
+            live = jnp.where(lane < cntb[rows, :], cur[rows, :].astype(F32), 0.0)
+            lf[pl.ds(PITCH * (i + 2) + 8, 2 * TY), :] = live
+        for i in range(2 * low_p, 2 * high_p):
+            for k in (1, 2):
+                plane(i + 2, k)
+        if part == 0:
+            loads[2].wait()
+        count = high_p - low_p
+        lhs = lines(ll, 2 + 2 * low_p, 2 * count, 1, 2)
+        pv[pl.ds(64 * low_p, 64 * count), :] = jnp.dot(lhs, agg[...], preferred_element_type=F32).astype(BF16)
+        if part == 0:
+            loads[3].wait()
+        total = jnp.zeros((16 * count, 512), F32)
+        for q in range(4):
+            child = jnp.concatenate([pv[pl.ds(64 * p + 16 * q, 16), :] for p in range(low_p, high_p)], axis=0)
+            total = total + jnp.dot(child, c2p[pl.ds(256 * q, 256), :], preferred_element_type=F32)
+        own[pl.ds(16 * low_p, 16 * count), :] = total.astype(BF16)
+        if part == 0:
+            pl.semaphore_wait(barrier, 6)
+        for i in (2 * part, 2 * part + 1):
+            if part == 1:
+                go(x_copy(0, y, i, OWN[i], True))
+            for dr in range(2):
+                go(y_copy(dr, 0, 0, i, True))
+            if part == 0:
+                go(x_copy(0, y, i, OWN[i], True))
 
     def x_halo(k):
         src = (2, 3, TX, TX + 1)[k]
@@ -235,11 +230,13 @@
 
     def unfold(sl, src, first, count):
         def line(p, _):
-            rows = src[pl.ds(pl.multiple_of(64 * p, 64), 64), :].astype(F32)
-            tiles[pl.ds(pl.multiple_of(1024 * p + 64 * sl, 64), 64), :] = rows
+            rows = src[pl.ds(pl.multiple_of(16 * p, 16), 16), :].astype(F32)
+            base = pl.multiple_of(1024 * p + 64 * sl, 64)
+            for q in range(4):
+                tiles[pl.ds(base + q, 16, stride=4), :] = rows[:, 128 * q : 128 * q + 128]
             return 0
 
-        lax.fori_loop(first // 64, (first + count) // 64, line, 0)
+        lax.fori_loop(first // 16, (first + count) // 16, line, 0)
 
     def unfold_slot(yy, xx, first, count):
         sl = slot(yy, xx)
@@ -323,7 +320,7 @@
                 for dr in turns(d, i):
                     go(y_copy(dr, d, 0, i))
         for dr in range(2 if d < 4 else 1):
-            unfold_slot(y - sign[dr] * d, xh, 0, ROWS)
+            unfold_slot(y - sign[dr] * d, xh, 0, CELLS)
 
     def other_step(d):
         for i in range(len(OTHER)):
@@ -336,16 +333,16 @@
                 for dr in turns(d, i):
                     go(y_copy(dr, d, 1, i))
         for dr in range(2 if 0 < d < 4 else 1):
-            unfold_slot(y - sign[dr] * d, px, 0, FIRST)
+            unfold_slot(y - sign[dr] * d, px, LATER, CELLS - LATER)
 
     def cross_step(d):
         for i in range(2):
             for dr in (0,) if d == 0 else turns(d - 1, i):
                 x_arrival(number(d, dr), y - sign[dr] * d, i, OWN[i]).wait_recv()
         for dr in range(2 if 0 < d < 4 else 1):
-            unfold_slot(y - sign[dr] * d, px, FIRST, ROWS - FIRST)
-
-    unfold(gy, own, 0, ROWS)
+            unfold_slot(y - sign[dr] * d, px, 0, LATER)
+
+    unfold(gy, own, 0, CELLS)
     for e in range(4):
         factor_part(e)
     own_step(1)
@@ -431,21 +428,29 @@
     for e in range(9, 12):
         factor_part(e)
     cross_step(2)
+    settled = len(sent)
     own_step(4)
     other_step(3)
     lax.fori_loop(TX // 2, TX, lower_line, 0)
     for e in range(12, 16):
         factor_part(e)
     cross_step(3)
+    for copy in sent[:settled]:
+        copy.wait_send()
     other_step(4)
     cross_step(4)
-    for copy in sent:
+    for copy in sent[settled:]:
         copy.wait_send()
 
 
-def finish_kernel(order, tiles, factor_r, factor_i, low_v, near_v, mask_v, p2c_in, recv_in, result, sums, incoming, p2c, recv_map, out, sem):
+def finish_kernel(order_in, tiles, factor_r, factor_i, low_v, near_v, mask_v, p2c_in, recv_in, result, sums, incoming, p2c, recv_map, out, order, sem):
+    few, rest = pl.ds(0, 8), pl.ds(8, 24)
+    lists = [
+        pltpu.make_async_copy(order_in.at[few], order.at[few], sem.at[6]),
+        pltpu.make_async_copy(order_in.at[rest], order.at[rest], sem.at[7]),
+    ]
     loads = [pltpu.make_async_copy(p2c_in, p2c, sem.at[0]), pltpu.make_async_copy(recv_in, recv_map, sem.at[1])]
-    for copy in loads:
+    for copy in lists + loads:
         copy.start()
 
     def targets(n, _):
@@ -462,7 +467,10 @@
             sums[pl.ds(rows + 4, 4), :] = second
         return 0
 
-    lax.fori_loop(0, 32, targets, 0)
+    lists[0].wait()
+    lax.fori_loop(0, 8, targets, 0)
+    lists[1].wait()
+    lax.fori_loop(8, 32, targets, 0)
 
     def take(row):
         return sums[pl.ds(row, 256, stride=8), :]
@@ -538,7 +546,7 @@
             vmem((256, 16), jnp.int32),
             vmem((16, 16), jnp.int32),
             vmem((256, 16), jnp.int32),
-            vmem((n_gy, ROWS, 128), BF16),
+            vmem((n_gy, CELLS, 512), BF16),
             vmem((192, 512), BF16),
             vmem((256, 16), F32),
             vmem((2048, 32), BF16),
@@ -547,8 +555,7 @@
             vmem((WIDE * PITCH, 128), F32),
             vmem((WIDE * 64, 256), BF16),
             vmem((1024, 256), BF16),
-            vmem((ROWS, 128), F32),
-            vmem((ROWS, 128), BF16),
+            vmem((CELLS, 512), BF16),
             vmem((WIDE * 8, 128), BF16),
             vmem((WIDE * 8, 128), BF16),
             vmem((WIDE * 8, 128), BF16),
@@ -585,7 +592,7 @@
         finish_kernel,
         name="finish",
         out_shape=jax.ShapeDtypeStruct((2048, 128), F32),
-        in_specs=[pl.BlockSpec(memory_space=pltpu.SMEM)] + [near_by] * 6 + [held] * 2,
+        in_specs=[near_by] * 7 + [held] * 2,
         out_specs=held,
         scratch_shapes=[
             vmem((2048, 128), F32),
@@ -593,7 +600,8 @@
             vmem((2048, 256), BF16),
             vmem((256, 256), BF16),
             vmem((2048, 128), F32),
-            pltpu.SemaphoreType.DMA((6,)),
+            pltpu.SMEM((32, 128), jnp.int32),
+            pltpu.SemaphoreType.DMA((8,)),
         ],
         compiler_params=pltpu.CompilerParams(vmem_limit_bytes=6 * 1024 * 1024),
     )(

time: 54.6 us -> 54.3 us (level)
  no operation moved by 1% of the time
where the time goes in v4:
time: 54.3 us; the launch traced here: 54.1 us
  Pallas kernels  54.1 us (100%)
    pallas_call x1, Pallas kernels, body(): pl.pallas_call(functools.partial(gather_kernel, n_gx, n_gy), name='gather...  46.9 us
    pallas_call x1, Pallas kernels, body(): pl.pallas_call(finish_kernel, name='finish', out_shape=jax.ShapeDtypeStru...  7.18 us

profile of v4, /device:TPU:8, one launch (start us, length us, event | category | flops | bytes accessed | tf_op | source)
XLA Modules:
  0.0 54.1 jit_solution(4370804577490570408)
XLA Ops:
  0.0 46.9 %gather.1 = (s32[32,128]{1,0:T(8,128)S(1)}, f32[16384,128]{1,0:T(8,128)S(1)}, f32[16384,128]{1,0:T(8,128)S(1)}, f32[16384,128]{1,0:T(8,128)S(1)}, f32[1024,256]{...) custom-call(bf16[2048,128]{1,0:T(8,128)(2,1)} %bitcast.22, s32[32,32]{1,0:T(8,128)} %cnt_in.1, ...), custom_call_target="tpu_custom_call" | custom-call | tf_op jit(solution)/shard_map/gather/pallas_call | solution.py:524
  46.9 7.2 %finish.1 = f32[2048,128]{1,0:T(8,128)} custom-call(s32[32,128]{1,0:T(8,128)S(1)} %get-tuple-element.12.order_in, f32[4096,4,128]{2,1,0:T(4,128)S(1)} %bitcast.16, f32[4096,4,128]{2,1,0:T(4,128)S(1)} %bitcast.17, f32[4096,4,128]{2,1,0:T(4,128)S(1)} %bitcast.18, f32[1024,256]{1,0:T(8,128)S(1)} %get-tuple-element.16.low_v, ...), custom_call_target="tpu_custom_call" | custom-call | tf_op jit(solution)/shard_map/finish/pallas_call | solution.py:591
